TPU v7x, 128 devices: a whole 4x4x4 slice. The times are simulated.
128 devices in a mesh: sys: 8 (over z_hi, x), edge: 16 (over y, z_lo, core).
Axes of the slice: x: 4, y: 4, z: 4 (z_hi: 2, z_lo: 2; z = z_hi * 2 + z_lo), core: 2. Of those that a mesh axis runs over, the one named last changes fastest.
Arguments:
- atoms: bfloat16 [8, 1024, 896], P('sys', 'edge'), may hold values from -6 to 6
- cotangent: bfloat16 [8, 1024, 896], P('sys', 'edge'), may hold values from -6 to 6
- experts: bfloat16 [32, 1792, 896], P('sys', 'edge'), may hold values from -0.125 to 0.125
- radial: bfloat16 [8, 32768, 896], P('sys', 'edge'), may hold values from -6 to 6
- coef: float32 [8, 32], replicated, may hold values from 0.02 to 0.5
- source: int32 [8, 32768], P('sys', 'edge'), may hold values from 0 to 1023
- target: int32 [8, 32768], P('sys', 'edge'), may hold values from 0 to 1023
Outputs:
- node_out: bfloat16 [8, 1024, 896], P('sys', 'edge')
- atom_grad: float32 [8, 1024, 896], P('sys', 'edge')
- expert_grad: float32 [32, 1792, 896], P('sys', 'edge')
All inputs are finite; a program needn't handle non-finite values.
Results may differ from a plain program's by a relative error of at most 0.018.
Values may be sent and summed in bfloat16 or wider, within the bound.
A program may use at most 128 MiB of HBM per device.

v0:
```python
import jax
import jax.numpy as jnp
from jax import lax
from jax.sharding import Mesh
from jax.sharding import PartitionSpec as P

SYS = ("sys_0", "sys_1")


def side_by_side(arrays, axis, dim, along):
    both = jnp.concatenate(arrays, axis=along)
    filled, at, done = (lax.all_gather(both, axis, axis=dim, tiled=True), 0, [])
    for a in arrays:
        done.append(lax.slice_in_dim(filled, at, at + a.shape[along], axis=along))
        at += a.shape[along]
    return tuple(done)


def side_by_side_2(arrays, axis, dim, along):
    widths = [a.shape[along] for a in arrays]
    both = jnp.concatenate(arrays, axis=along)
    filled = lax.psum_scatter(both, axis, scatter_dimension=dim, tiled=True)
    return tuple(jnp.split(filled, [sum(widths[:k]) for k in range(1, len(widths))], axis=along))


def joined_along(parts, dim):
    dims = list(parts.shape[1:])
    dims[dim] *= parts.shape[0]
    return jnp.moveaxis(parts, 0, dim).reshape(dims)


def gather_in_order(x, axes, sequence):
    parts = x
    for k in sequence:
        parts = lax.all_gather(parts, axes[k])
    done = sequence[::-1]
    back = [done.index(k) for k in range(len(axes))]
    parts = parts.transpose(*back, *range(len(axes), parts.ndim))
    return parts.reshape(-1, *x.shape)


def whole_of(x, axes, sequence, dim):
    return joined_along(gather_in_order(x, axes, sequence), dim)


def shards(atoms, cotangent, experts, radial, coef, source, target):
    sys_index = lax.axis_index(SYS)
    exp_dev = experts.shape[0]
    width = experts.shape[2]
    highest = lax.Precision.HIGHEST
    all_atoms, all_cot = side_by_side((atoms[0], cotangent[0]), "edge", 0, 1)
    atom_total = all_atoms.shape[0]
    own_coef = lax.dynamic_slice_in_dim(coef, sys_index * exp_dev, exp_dev, 1)
    own_experts = experts.astype(jnp.float32)
    chosen = own_coef
    merged_part = lax.psum_scatter(
        jnp.einsum("se,erd->srd", chosen, own_experts, precision=highest),
        SYS,
        scatter_dimension=0,
        tiled=True,
    )[0]
    merged_rows = merged_part.astype(jnp.bfloat16)
    src_idx = source[0]
    tgt_idx = target[0]
    edge_in = jnp.concatenate(
        [jnp.take(all_atoms, src_idx, axis=0), jnp.take(all_atoms, tgt_idx, axis=0)], axis=1
    )
    full_weight = lax.all_gather(merged_rows, "edge", axis=0, tiled=True)
    pre = jnp.dot(edge_in, full_weight, preferred_element_type=jnp.float32)
    radial_f = radial[0].astype(jnp.float32)
    message = (jax.nn.silu(pre) * radial_f).astype(jnp.bfloat16)
    node_part = jax.ops.segment_sum(message.astype(jnp.float32), tgt_idx, num_segments=atom_total)
    edge_cot = jnp.take(all_cot, tgt_idx, axis=0).astype(jnp.float32)
    sigma = jax.nn.sigmoid(pre)
    slope = sigma * (1.0 + pre * (1.0 - sigma))
    pre_grad = (edge_cot * radial_f * slope).astype(jnp.bfloat16)
    input_grad = lax.dot_general(
        pre_grad, full_weight, (((1,), (1,)), ((), ())), preferred_element_type=jnp.float32
    )
    input_grad = input_grad.astype(jnp.bfloat16)
    grad_part = jax.ops.segment_sum(
        input_grad[:, :width].astype(jnp.float32), src_idx, num_segments=atom_total
    )
    grad_part = grad_part + jax.ops.segment_sum(
        input_grad[:, width:].astype(jnp.float32), tgt_idx, num_segments=atom_total
    )
    node_sum, grad_sum = side_by_side_2((node_part, grad_part), "edge", 0, 1)
    merged_grad = lax.psum_scatter(
        lax.dot_general(
            edge_in, pre_grad, (((0,), (0,)), ((), ())), preferred_element_type=jnp.float32
        ),
        "edge",
        scatter_dimension=0,
        tiled=True,
    )
    piece = whole_of(merged_grad[None], SYS, (0, 1), 0)
    chosen = lax.dynamic_slice(coef, (0, sys_index * exp_dev), (piece.shape[0], exp_dev))
    expert_grad = jnp.einsum("se,srd->erd", chosen, piece, precision=highest)
    return (node_sum.astype(jnp.bfloat16)[None], grad_sum[None], expert_grad)


def solution(mesh):
    finer = Mesh(mesh.devices.reshape(2, 4, mesh.shape["edge"]), ("sys_0", "sys_1", "edge"))
    return jax.shard_map(
        shards,
        mesh=finer,
        in_specs=(
            P(SYS, "edge", None),
            P(SYS, "edge", None),
            P(SYS, "edge", None),
            P(SYS, "edge", None),
            P(),
            P(SYS, "edge"),
            P(SYS, "edge"),
        ),
        out_specs=(P(SYS, "edge", None), P(SYS, "edge", None), P(SYS, "edge", None)),
        check_vma=False,
    )
```

profile of v0, /device:TPU:1, one launch (start us, length us, event | category | flops | bytes accessed | tf_op | source)
XLA Modules:
  0.0 369.4 jit_solution(8873350030532675640)
XLA Ops:
  8.0 0.0 copy-start
  8.0 0.0 reduce-scatter.4.cloned.1.call-start
  8.1 1.1 copy-done
  9.1 2.3 fusion.19
  11.4 0.0 copy-start.5
  11.4 0.0 copy-start.6
  11.4 2.3 copy.20
  13.7 0.0 copy-start.8
  13.7 0.0 copy-start.7
  13.7 0.0 reduce-scatter.4.cloned.1.call-update
  13.7 0.0 all-gather.7.cloned.1.call-start
  13.8 0.0 copy-done.5
  13.8 0.0 copy-done.6
  13.8 0.7 pad_maximum_fusion.4
  14.5 0.0 all-gather.7.cloned.1.call-update
  14.5 0.0 all-gather.9.cloned.1.call-start
  14.6 85.3 %reduce-scatter.4.cloned.1.call-done = f32[1,112,896]{2,1,0:T(8,128)} async-done(((f32[8,112,896]{2,1,0:T(8,128)}), f32[1,112,896]{2,1,0:T(8,128)}) %reduce-scatter.4.cloned.1.call-update) | async-done | bytes 401424 | tf_op jit(solution)/shard_map/reduce_scatter | solution.py:56
  99.8 1.7 convert_element_type.35
  101.5 0.0 all-gather.9.cloned.1.call-update
  101.6 0.0 reduce-scatter.8.cloned.1.call-start
  101.6 0.0 copy-done.8
  101.6 0.0 copy-done.7
  101.7 0.0 all-gather.7.cloned.1.call-done
  101.7 3.6 fusion.33
  105.3 12.3 %gather_fusion.2 = bf16[2048,896]{1,0:T(8,128)(2,1)} fusion(bf16[1024,896]{1,0:T(8,128)(2,1)} %get-tuple-element.13, s32[2048]{0:T(1024)S(1)} %fusion.23), kind=kCustom, calls=%fused_computation.2.clone | custom fusion | bytes 7348224 | tf_op jit(solution)/shard_map/jit(_take)/gather | solution.py:73
  117.6 9.5 %gather_fusion.1 = bf16[2048,896]{1,0:T(8,128)(2,1)} fusion(bf16[1024,896]{1,0:T(8,128)(2,1)S(1)} %get-tuple-element.14, s32[2048]{0:T(1024)S(1)} %fusion.23), kind=kCustom, calls=%fused_computation.1.clone | custom fusion | bytes 7348224 | tf_op jit(solution)/shard_map/jit(_take)/gather | solution.py:66
  127.1 9.5 %gather_fusion = bf16[2048,896]{1,0:T(8,128)(2,1)} fusion(bf16[1024,896]{1,0:T(8,128)(2,1)S(1)} %get-tuple-element.14, s32[2048]{0:T(1024)S(1)} %fusion.22), kind=kCustom, calls=%fused_computation.clone | custom fusion | bytes 7348224 | tf_op jit(solution)/shard_map/jit(_take)/gather | solution.py:66
  136.6 5.6 %broadcast_select_fusion = (bf16[2048,896]{1,0:T(8,128)(2,1)}, bf16[2048,896]{1,0:T(8,128)(2,1)}) fusion(bf16[2048,896]{1,0:T(8,128)(2,1)} %gather_fusion.1, pred[2048]{0:T(1024)(128)(4,1)S(1)} %compare_and_fusion, bf16[2048,896]{1,0:T(8,128)(2,1)} %gather_fusion, pred[2048]{0:T(1024)(128)(4,1)S(1)} %compare_and_fusion.1), kind=kLoop, calls=%fused_computation.25 | loop fusion | flops 3670016 | bytes 14684160 | tf_op jit(solution)/shard_map/jit(_take)/select_n | solution.py:66
  142.3 0.0 all-gather.9.cloned.1.call-done
  142.3 0.0 copy-start.3
  142.3 0.0 copy-start.4
  142.3 15.8 %fusion.2 = (bf16[2048,896]{1,0:T(8,128)(2,1)S(1)}, f32[2048,896]{1,0:T(8,128)}) fusion(bf16[1,2048,896]{2,1,0:T(8,128)(2,1)} %param.12, bf16[2048,896]{1,0:T(8,128)(2,1)} %gather_fusion.2, pred[2048]{0:T(1024)(128)(4,1)S(1)} %compare_and_fusion, bf16[1,1792,896]{2,1,0:T(8,128)(2,1)} %all-gather.9.cloned.1.call-done, ...), kind=kOutput, calls=%fused_computation.11 | convolution fusion | flops 6615203840 | bytes 28903424 | tf_op jit(solution)/shard_map/dot_general | solution.py:69
  158.1 0.0 copy-start.10
  158.1 1.8 copy-done.10
  159.9 0.0 copy-done.3
  159.9 0.0 copy-done.4
  159.9 9.9 %fusion.9 = f32[1792,896]{1,0:T(8,128)} fusion(bf16[2048,896]{1,0:T(8,128)(2,1)S(1)} %get-tuple-element.15, bf16[2048,896]{1,0:T(8,128)(2,1)S(1)} %copy-done.3, bf16[2048,896]{1,0:T(8,128)(2,1)S(1)} %copy-done.4), kind=kOutput, calls=%fused_computation.21 | convolution fusion | flops 6591348736 | bytes 17432576 | tf_op jit(solution)/shard_map/dot_general | solution.py:89
  169.8 0.0 reduce-scatter.8.cloned.1.call-update
  169.9 0.2 reduce-scatter.6.cloned.1.call-start
  170.1 12.4 %convolution_convert_fusion = bf16[2048,1792]{1,0:T(8,128)(2,1)} fusion(bf16[2048,896]{1,0:T(8,128)(2,1)} %copy-done.10, bf16[1,1792,896]{2,1,0:T(8,128)(2,1)} %all-gather.9.cloned.1.call-done), kind=kOutput, calls=%fused_computation.8 | convolution fusion | flops 6580338688 | bytes 14221312 | tf_op jit(solution)/shard_map/dot_general | solution.py:77
  182.5 20.1 %scatter_custom_fusion.2 = f32[1024,896]{1,0:T(8,128)} fusion(s32[2048]{0:T(1024)S(1)} %bitcast.51, bf16[2048,1792]{1,0:T(8,128)(2,1)} %convolution_convert_fusion, f32[]{:T(128)} %constant.9.clone.1), kind=kCustom, calls=%fused_computation.14 | custom fusion | flops 3670016 | bytes 7340544 | tf_op jit(solution)/shard_map/scatter-add | solution.py:84
  202.5 20.0 %scatter_custom_fusion.1 = f32[1024,896]{1,0:T(8,128)} fusion(s32[2048]{0:T(1024)S(1)} %bitcast.48, bf16[2048,1792]{1,0:T(8,128)(2,1)} %convolution_convert_fusion, f32[]{:T(128)} %constant.9.clone.1), kind=kCustom, calls=%fused_computation.16 | custom fusion | flops 3670016 | bytes 7340544 | tf_op jit(solution)/shard_map/scatter-add | solution.py:81
  222.5 22.2 %scatter_custom_fusion = f32[1024,896]{1,0:T(8,128)} fusion(s32[2048]{0:T(1024)S(1)} %bitcast.52, f32[2048,896]{1,0:T(8,128)} %get-tuple-element.16, bf16[1,2048,896]{2,1,0:T(8,128)(2,1)} %param.12, f32[]{:T(128)} %constant.33.clone.1, f32[]{:T(128)} %constant.9.clone.1), kind=kCustom, calls=%fused_computation.18 | custom fusion | flops 16515072 | bytes 14680072 | tf_op jit(solution)/shard_map/scatter-add | solution.py:72
  244.7 0.0 copy-start.2
  244.7 3.7 %add.40 = f32[1024,896]{1,0:T(8,128)S(1)} add(f32[1024,896]{1,0:T(8,128)} %scatter_custom_fusion.1, f32[1024,896]{1,0:T(8,128)} %scatter_custom_fusion.2) | non-fusion elementwise | flops 917504 | bytes 11010048 | tf_op jit(solution)/shard_map/add | solution.py:84
  248.4 0.6 copy-done.2
  249.0 3.5 pad_maximum_fusion.1
  252.5 0.0 reduce-scatter.6.cloned.1.call-update
  252.6 0.0 all-gather.11.cloned.1.call-start
  252.6 0.0 reduce-scatter.8.cloned.1.call-done
  252.6 11.2 %all-gather.1 = f32[224,896]{1,0:T(8,128)} all-gather(f32[112,896]{1,0:T(8,128)} %reduce-scatter.8.cloned.1.call-done), channel_id=3, replica_groups=mesh['sys_0'=2,'sys_1'=4,'edge'=16] {'sys_0'}, dimensions={0}, use_global_device_ids=true | all-gather | bytes 1204224 | tf_op jit(solution)/shard_map/all_gather | solution.py:35
  263.8 0.0 all-gather.11.cloned.1.call-update
  263.9 78.2 %reduce-scatter.6.cloned.1.call-done = f32[64,1792]{1,0:T(8,128)} async-done(((f32[1024,1792]{1,0:T(8,128)}), f32[64,1792]{1,0:T(8,128)}) %reduce-scatter.6.cloned.1.call-update) | async-done | bytes 458768 | tf_op jit(solution)/shard_map/reduce_scatter | solution.py:22
  342.0 1.6 fusion.21
  343.6 1.6 slice_bitcast_fusion
  345.3 0.0 all-gather.11.cloned.1.call-done
  345.3 5.6 %copy.28 = f32[4,2,1,112,896]{4,0,1,3,2:T(4,128)} copy(f32[4,2,1,112,896]{4,3,1,0,2:T(8,128)} %bitcast.42) | data formatting | bytes 6422528 | tf_op jit(solution)/shard_map/all_gather | solution.py:35
  350.9 0.0 copy-start.9
  350.9 0.0 copy-start.1
  350.9 5.1 %reshape_reshape.3 = f32[8,112,896]{2,0,1:T(8,128)} reshape(f32[2,4,1,112,896]{4,1,0,3,2:T(4,128)} %bitcast.41) | data formatting | bytes 6422528 | tf_op jit(solution)/shard_map/reshape;reshape | solution.py:29
  356.0 0.0 copy-done.9
  356.0 4.5 %fusion.24 = f32[4,112,896]{2,0,1:T(4,128)S(1)} fusion(f32[8,112,896]{2,0,1:T(8,128)} %reshape_reshape.3, f32[8,32]{1,0:T(8,128)S(1)} %copy-done.9, s32[]{:T(128)S(6)} %select_n.11), kind=kOutput, calls=%fused_computation.45 | convolution fusion | flops 38535168 | bytes 4817924 | tf_op jit(solution)/shard_map/se,srd->erd/dot_general | solution.py:98
  360.6 1.3 copy.23
  361.8 0.0 copy-done.1
  (4 shorter events, 0.0 us)
Async XLA Ops:
  8.0 1.1 copy-start
  8.0 91.8 %reduce-scatter.4.cloned.1.call-start = ((), (), s32[]{:S(2)}) async-start(), calls=%async_computation.4 | async-start | bytes 3612672 | tf_op jit(solution)/shard_map/reduce_scatter | solution.py:56
  11.4 2.4 copy-start.5
  11.4 2.4 copy-start.6
  13.7 87.9 %copy-start.8 = (s32[1,2048]{1,0:T(1,128)S(1)}, s32[1,2048]{1,0:T(1,128)}, u32[]{:S(2)}) copy-start(s32[1,2048]{1,0:T(1,128)} %param.15) | copy-start | bytes 24580
  13.7 88.0 %copy-start.7 = (s32[1,2048]{1,0:T(1,128)S(1)}, s32[1,2048]{1,0:T(1,128)}, u32[]{:S(2)}) copy-start(s32[1,2048]{1,0:T(1,128)} %param.14) | copy-start | bytes 24580
  13.7 88.0 %all-gather.7.cloned.1.call-start = ((), (), s32[]{:S(2)}) async-start(), calls=%async_computation.3 | async-start | bytes 3899392 | tf_op jit(solution)/shard_map/all_gather | solution.py:12
  14.5 127.7 %all-gather.9.cloned.1.call-start = ((), (), s32[]{:S(2)}) async-start(), calls=%async_computation.7 | async-start | bytes 3411968 | tf_op jit(solution)/shard_map/all_gather | solution.py:68
  101.6 151.1 %reduce-scatter.8.cloned.1.call-start = ((), (), s32[]{:S(2)}) async-start(), calls=%async_computation.6 | async-start | bytes 6823936 | tf_op jit(solution)/shard_map/reduce_scatter | solution.py:88
  142.3 17.6 %copy-start.3 = (bf16[2048,896]{1,0:T(8,128)(2,1)S(1)}, bf16[2048,896]{1,0:T(8,128)(2,1)}, u32[]{:S(2)}) copy-start(bf16[2048,896]{1,0:T(8,128)(2,1)} %get-tuple-element.17) | copy-start | bytes 11010052
  142.3 17.6 %copy-start.4 = (bf16[2048,896]{1,0:T(8,128)(2,1)S(1)}, bf16[2048,896]{1,0:T(8,128)(2,1)}, u32[]{:S(2)}) copy-start(bf16[2048,896]{1,0:T(8,128)(2,1)} %get-tuple-element.18) | copy-start | bytes 11010052
  158.1 1.8 copy-start.10
  169.9 172.2 %reduce-scatter.6.cloned.1.call-start = ((), (), s32[]{:S(2)}) async-start(), calls=%async_computation.5 | async-start | bytes 7798784 | tf_op jit(solution)/shard_map/reduce_scatter | solution.py:22
  244.7 4.3 %copy-start.2 = (f32[1024,896]{1,0:T(8,128)S(1)}, f32[1024,896]{1,0:T(8,128)}, u32[]{:S(2)}) copy-start(f32[1024,896]{1,0:T(8,128)} %scatter_custom_fusion) | copy-start | bytes 11010052
  252.6 92.7 %all-gather.11.cloned.1.call-start = ((), (), s32[]{:S(2)}) async-start(), calls=%async_computation.8 | async-start | bytes 4014080 | tf_op jit(solution)/shard_map/all_gather | solution.py:35
  350.9 5.1 %copy-start.9 = (f32[8,32]{1,0:T(8,128)S(1)}, f32[8,32]{1,0:T(8,128)}, u32[]{:S(2)}) copy-start(f32[8,32]{1,0:T(8,128)} %param.13) | copy-start | bytes 3076
  350.9 10.9 %copy-start.1 = (bf16[4,112,896]{2,1,0:T(8,128)(2,1)S(1)}, bf16[4,112,896]{2,1,0:T(8,128)(2,1)}, u32[]{:S(2)}) copy-start(bf16[4,112,896]{2,1,0:T(8,128)(2,1)} %param.11) | copy-start | bytes 2408452
Sparse Core Ops, SparseCore 0:
  13.8 85.9 reduce-scatter.3
  264.0 49.2 all-gather.10
Sparse Core Ops, SparseCore 1:
  16.5 43.8 all-gather.6
  101.7 36.1 all-gather.8
  169.9 78.1 reduce-scatter.7
  252.6 89.3 reduce-scatter.5
where the time goes:
time: 370 us; the launch traced here: 369 us
  waiting for transfers between devices  164 us (44%)
  other arithmetic  77.5 us (21%)
  local copies, waits for them, and re-layouts  55.9 us (15%)
  matrix products  44.9 us (12%)
  between operations  15.8 us (4%)
  blocking collectives  11.2 us (3%)
    reduce_scatter x1, waiting for transfers between devices, shards(): lax.psum_scatter(jnp.einsum('se,erd->srd', chosen, own_experts, precision...  85.3 us
    reduce_scatter x1, waiting for transfers between devices, side_by_side_2(): filled = lax.psum_scatter(both, axis, scatter_dimension=dim, tiled=True)  78.2 us
    scatter-add x1, other arithmetic, shards(): jax.ops.segment_sum(message.astype(jnp.float32), tgt_idx, num_segments=at...  22.2 us
    scatter-add x1, other arithmetic, shards(): jax.ops.segment_sum(input_grad[:, width:].astype(jnp.float32), tgt_idx, n...  20.1 us
    scatter-add x1, other arithmetic, shards(): jax.ops.segment_sum(input_grad[:, :width].astype(jnp.float32), src_idx, n...  20 us
    dot_general x1, matrix products, shards(): pre = jnp.dot(edge_in, full_weight, preferred_element_type=jnp.float32)  15.8 us
    dot_general x1, matrix products, shards(): lax.dot_general(pre_grad, full_weight, (((1,), (1,)), ((), ())), preferre...  12.4 us
    gather x1, local copies, waits for them, and re-layouts, shards(): edge_cot = jnp.take(all_cot, tgt_idx, axis=0).astype(jnp.float32)  12.3 us
  transfers between devices with their start and end apart: 6, of which 2 were waited for; matrix products, arithmetic and copies ran while one was open for 35% of the time, Pallas kernels for 0%

commit v1 on v0

v1 whole, which is shorter than its diff:
```python
import functools

import jax
import jax.numpy as jnp
from jax import lax
from jax.experimental import pallas as pl
from jax.experimental.pallas import tpu as pltpu
from jax.sharding import PartitionSpec as P

F32 = jnp.float32
BF16 = jnp.bfloat16
MESH = pl.DeviceIdType.MESH
NX, NY = 4, 4
SHIFTS = (2, 1, 3)
SYS_STEPS = tuple((dz, dx) for dx in (2, 1, 3, 0) for dz in (1, 0) if (dz, dx) != (0, 0))


def dot(a, b):
    return lax.dot_general(a, b, (((1,), (0,)), ((), ())), preferred_element_type=F32)


def dot_t(a, b):
    return lax.dot_general(a, b, (((1,), (1,)), ((), ())), preferred_element_type=F32)


def kernel(
    chunks,
    experts,
    coef,
    atoms,
    cot,
    radial_hbm,
    src_rows,
    tgt_rows,
    src_line,
    tgt_line,
    node_out,
    atom_grad,
    expert_grad,
    radial,
    at_all,
    ct_all,
    oh_src,
    oh_tgt,
    ot_src,
    ot_tgt,
    sel_atoms,
    proj,
    edge_vals,
    per_chunk,
    local_sem,
    send_sem,
    recv_sem,
):
    n_exp, rows, width = experts.shape
    own_atoms = atoms.shape[0]
    n_atoms = 16 * own_atoms
    n_edges = radial.shape[0]
    n_sys = 2 * NX
    sys_id = lax.axis_index("sys")
    edge_id = lax.axis_index("edge")
    zh, x = sys_id // NX, sys_id % NX
    y, zl, c = edge_id // 4, (edge_id // 2) % 2, edge_id % 2
    plane = y * 2 + zl

    def sys_peer(dz, dx):
        return (((zh + dz) % 2) * NX + (x + dx) % NX, edge_id)

    def y_peer(d):
        return (sys_id, ((y + d) % NY) * 4 + zl * 2 + c)

    z_peer = (sys_id, y * 4 + (1 - zl) * 2 + c)
    c_peer = (sys_id, y * 4 + zl * 2 + (1 - c))

    radial_copy = pltpu.make_async_copy(radial_hbm, radial, local_sem.at[0])
    radial_copy.start()

    barrier = pltpu.get_barrier_semaphore()
    peers = [sys_peer(dz, dx) for dz, dx in SYS_STEPS] + [y_peer(d) for d in SHIFTS] + [z_peer, c_peer]
    for p in peers:
        pl.semaphore_signal(barrier, inc=1, device_id=p, device_id_type=MESH)
    pl.semaphore_wait(barrier, len(peers))

    sent = []

    def send(src, dst, peer):
        i = len(sent)
        cp = pltpu.make_async_remote_copy(
            src_ref=src,
            dst_ref=dst,
            send_sem=send_sem.at[i],
            recv_sem=recv_sem.at[i],
            device_id=peer,
            device_id_type=MESH,
        )
        cp.start()
        sent.append(cp)
        return cp

    at_all[pl.ds(plane, 1), pl.ds(c, 1)] = atoms[...][None, None]
    ct_all[pl.ds(plane, 1), pl.ds(c, 1)] = cot[...][None, None]
    pairs = ((atoms, at_all), (cot, ct_all))
    a_z = [send(own, full.at[plane, c], z_peer) for own, full in pairs]
    a_y = [send(own, full.at[plane, c], y_peer(d)) for own, full in pairs for d in SHIFTS]

    e_recv = [None] * len(chunks)

    def expert_part(k):
        start, size = chunks[k]
        b = per_chunk[k]
        e_recv[k] = []
        for i, (dz, dx) in enumerate(SYS_STEPS + ((0, 0),)):
            to = ((zh + dz) % 2) * NX + (x + dx) % NX
            total = jnp.zeros((rows, size), F32)
            for e in range(n_exp):
                total += coef[to, sys_id * n_exp + e] * experts[e, :, start : start + size].astype(F32)
            b["epart"][i] = total.astype(BF16)
            if (dz, dx) != (0, 0):
                e_recv[k].append(send(b["epart"].at[i], b["erecv"].at[i], sys_peer(dz, dx)))

    m_z, m_y, m_f = ([None] * len(chunks) for _ in range(3))

    def merge(k):
        b = per_chunk[k]
        for cp in e_recv[k]:
            cp.wait_recv()
        total = b["epart"][n_sys - 1].astype(F32)
        for i in range(n_sys - 1):
            total += b["erecv"][i].astype(F32)
        b["merged"][pl.ds(plane, 1), pl.ds(c, 1)] = total.astype(BF16)[None, None]
        own = b["merged"].at[plane, c]
        m_z[k] = send(own, own, z_peer)
        m_y[k] = [send(own, own, y_peer(d)) for d in SHIFTS]

    def merge_forward(k):
        m_z[k].wait_recv()
        other = per_chunk[k]["merged"].at[y * 2 + 1 - zl, c]
        m_f[k] = [send(other, other, y_peer(d)) for d in SHIFTS]

    def merge_finish(k):
        for cp in m_y[k] + m_f[k]:
            cp.wait_recv()
        half = per_chunk[k]["merged"].at[:, c]
        send(half, half, c_peer).wait_recv()

    def one_hots():
        lane = lax.broadcasted_iota(jnp.int32, (128, 128), 1)

        def by_edge(j, _):
            at = pl.ds(pl.multiple_of(j * 128, 128), 128)
            for idx, out in ((src_rows, oh_src), (tgt_rows, oh_tgt)):
                col = jnp.broadcast_to(idx[pl.ds(j, 1), :], (128, 128)).T
                for a in range(n_atoms // 128):
                    out[at, a * 128 : (a + 1) * 128] = jnp.where(col == lane + a * 128, 1.0, 0.0).astype(BF16)
            return 0

        lax.fori_loop(0, n_edges // 128, by_edge, 0)
        sub = lax.broadcasted_iota(jnp.int32, (64, n_edges), 0)

        def by_atom(j, _):
            at = pl.ds(pl.multiple_of(j * 64, 64), 64)
            for idx, out in ((src_line, ot_src), (tgt_line, ot_tgt)):
                line = jnp.broadcast_to(idx[...], (64, n_edges)) - j * 64
                out[at, :] = jnp.where(line == sub, 1.0, 0.0).astype(BF16)
            return 0

        lax.fori_loop(0, n_atoms // 64, by_atom, 0)

    def select_atoms():
        first = (edge_id % 8) * rows
        i = lax.broadcasted_iota(jnp.int32, (128, width), 0)
        j = lax.broadcasted_iota(jnp.int32, (128, width), 1)
        pick = jnp.where((j == i + first) & (i < rows), 1.0, 0.0).astype(BF16)
        sel_atoms[...] = dot_t(pick, at_all[...].reshape(n_atoms, width)).astype(BF16)

    def edges(k):
        start, size = chunks[k]
        b = per_chunk[k]
        cols = slice(start, start + size)

        def project(t, _):
            at = pl.ds(pl.multiple_of(t * 256, 256), 256)
            a = at_all[pl.ds(t * 2, 2)].reshape(256, width)
            for h in range(2):
                w = b["merged"][4 * h : 4 * h + 4].reshape(width, size)
                proj[h, at, 0:size] = dot(a, w).astype(BF16)
            return 0

        lax.fori_loop(0, n_atoms // 256, project, 0)

        def pick(t, _):
            at = pl.ds(pl.multiple_of(t * 512, 512), 512)
            o_s, o_t = oh_src[at, :], oh_tgt[at, :]
            pre = dot(o_s, proj[0, :, 0:size]) + dot(o_t, proj[1, :, 0:size])
            edge_cot = dot(o_t, ct_all[:, :, :, cols].reshape(n_atoms, size))
            r = radial[at, cols].astype(F32)
            g = 1.0 / (1.0 + jnp.exp(-pre))
            edge_vals[at, 0:size] = (edge_cot * r * (g * (1.0 + pre * (1.0 - g)))).astype(BF16)
            edge_vals[at, size : 2 * size] = (pre * g * r).astype(BF16)
            return 0

        lax.fori_loop(0, n_edges // 512, pick, 0)

    c_recv = [None] * len(chunks)

    def sums(k):
        size = chunks[k][1]
        b = per_chunk[k]
        c_recv[k] = []
        for d in SHIFTS + (0,):
            yy = (y + d) % NY
            at = pl.ds(pl.multiple_of(yy * 256, 256), 256)
            o_s, o_t = ot_src[at, :], ot_tgt[at, :]
            by_src = dot(o_s, edge_vals[:, 0:size]).astype(BF16)
            by_tgt = dot(o_t, edge_vals[:, 0 : 2 * size]).astype(BF16)
            for q in range(4):
                spot = (pl.ds(q % 2, 1), pl.ds(yy, 1), pl.ds(q // 2, 1))
                r = slice(q * own_atoms, (q + 1) * own_atoms)
                b["sums"][(*spot, slice(None), slice(0, size))] = by_src[r][None, None, None]
                b["sums"][(*spot, slice(None), slice(size, 3 * size))] = by_tgt[r][None, None, None]
            c_recv[k].append((d, send(b["sums"].at[1 - c, yy], b["csums"].at[yy], c_peer)))

    g_z, n_y, g_y, n_z, q_y, q_z, q_c, d_s = ([None] * len(chunks) for _ in range(8))

    def reduce_core(k):
        size = chunks[k][1]
        b = per_chunk[k]
        for d, cp in c_recv[k]:
            cp.wait_recv()
            yy = pl.ds((y + d) % NY, 1)
            both = b["sums"][pl.ds(c, 1), yy][0].astype(F32) + b["csums"][yy].astype(F32)
            b["chip"][yy] = both.astype(BF16)
        g_z[k] = send(b["chip"].at[:, 1 - zl, :, 0 : 2 * size], b["gz"], z_peer)
        n_y[k] = [
            send(b["chip"].at[(y + d) % NY, :, :, 2 * size : 3 * size], b["ny"].at[i], y_peer(d))
            for i, d in enumerate(SHIFTS)
        ]

    def reduce_z(k):
        size = chunks[k][1]
        b = per_chunk[k]
        g_z[k].wait_recv()
        own = b["chip"][:, pl.ds(zl, 1), :, 0 : 2 * size].reshape(NY, own_atoms, 2 * size)
        b["gsum"][...] = (own.astype(F32) + b["gz"][...].astype(F32)).astype(BF16)
        g_y[k] = [
            send(b["gsum"].at[(y + d) % NY], b["gy"].at[i], y_peer(d)) for i, d in enumerate(SHIFTS)
        ]

    def reduce_y(k):
        start, size = chunks[k]
        b = per_chunk[k]
        for cp in g_y[k]:
            cp.wait_recv()
        total = b["gsum"][pl.ds(y, 1)][0].astype(F32)
        for i in range(3):
            total += b["gy"][i].astype(F32)
        g = total.astype(BF16)
        b["gown"][0] = g[:, 0:size]
        b["gown"][1] = g[:, size : 2 * size]
        b["gall"][pl.ds(y, 1), pl.ds(zl, 1), pl.ds(c, 1)] = b["gown"][pl.ds(y // 2, 1)][None, None]
        q_y[k] = [
            send(b["gown"].at[((y + d) % NY) // 2], b["gall"].at[y, zl, c], y_peer(d)) for d in SHIFTS
        ]
        grad = dot_t(g[:, 0:size], b["merged"][0:4].reshape(width, size))
        grad += dot_t(g[:, size : 2 * size], b["merged"][4:8].reshape(width, size))
        if k == 0:
            atom_grad[...] = grad
        else:
            atom_grad[...] += grad

    def node_z(k):
        size = chunks[k][1]
        b = per_chunk[k]
        for cp in n_y[k]:
            cp.wait_recv()
        total = b["chip"][pl.ds(y, 1), :, :, 2 * size : 3 * size][0].astype(F32)
        for i in range(3):
            total += b["ny"][i].astype(F32)
        b["nsum"][...] = total.astype(BF16)
        n_z[k] = send(b["nsum"].at[1 - zl], b["nz"], z_peer)

    def node_finish(k):
        start, size = chunks[k]
        b = per_chunk[k]
        n_z[k].wait_recv()
        total = b["nsum"][pl.ds(zl, 1)][0].astype(F32) + b["nz"][...].astype(F32)
        node_out[:, start : start + size] = total.astype(BF16)

    def share_z(k):
        for cp in q_y[k]:
            cp.wait_recv()
        part = per_chunk[k]["gall"].at[:, zl, c]
        q_z[k] = send(part, part, z_peer)

    def share_c(k):
        q_z[k].wait_recv()
        part = per_chunk[k]["gall"].at[:, :, c]
        q_c[k] = send(part, part, c_peer)

    def weight_grad(k):
        size = chunks[k][1]
        b = per_chunk[k]
        q_c[k].wait_recv()
        grad = dot(sel_atoms[...], b["gall"][...].reshape(n_atoms, size))
        b["dall"][pl.ds(sys_id, 1)] = grad[0:rows].astype(BF16)[None]
        own = b["dall"].at[sys_id]
        d_s[k] = [send(own, own, sys_peer(dz, dx)) for dz, dx in SYS_STEPS]

    def expert_finish(k):
        start, size = chunks[k]
        b = per_chunk[k]
        for cp in d_s[k]:
            cp.wait_recv()
        for e in range(n_exp):
            total = jnp.zeros((rows, size), F32)
            for s in range(n_sys):
                total += coef[s, sys_id * n_exp + e] * b["dall"][s].astype(F32)
            expert_grad[e, :, start : start + size] = total

    n = len(chunks)
    for k in range(n):
        expert_part(k)
    one_hots()
    for cp in a_z:
        cp.wait_recv()
    other = y * 2 + 1 - zl
    a_f = [send(full.at[other, c], full.at[other, c], y_peer(d)) for _, full in pairs for d in SHIFTS]
    merge(0)
    merge_forward(0)
    for cp in a_y + a_f:
        cp.wait_recv()
    a_c = [send(full.at[:, c], full.at[:, c], c_peer) for _, full in pairs]
    if n > 1:
        merge(1)
    for cp in a_c:
        cp.wait_recv()
    select_atoms()
    radial_copy.wait()
    if n > 1:
        merge_forward(1)
    merge_finish(0)

    def steps(k, half):
        if half == 0:
            todo = [(merge, k + 2), (reduce_z, k - 1), (share_z, k - 2), (expert_finish, k - 3)]
        else:
            todo = [
                (reduce_core, k),
                (merge_forward, k + 2),
                (merge_finish, k + 1),
                (reduce_y, k - 1),
                (node_z, k - 1),
                (share_c, k - 2),
                (weight_grad, k - 2),
                (node_finish, k - 2),
            ]
        for f, i in todo:
            if 0 <= i < n:
                f(i)

    for k in range(n + 3):
        if k < n:
            edges(k)
        steps(k, 0)
        if k < n:
            sums(k)
        steps(k, 1)
    for cp in sent:
        cp.wait_send()


def layer(atoms, cotangent, experts, radial, coef, source, target):
    n_exp, rows, width = experts.shape
    own = atoms.shape[1]
    n_atoms = 16 * own
    n_edges = radial.shape[1]
    chunks, at = [], 0
    while at < width:
        size = min(256, width - at)
        chunks.append((at, size))
        at += size

    def vmem(*shape):
        return pltpu.VMEM(shape, BF16)

    per_chunk = [
        {
            "epart": vmem(8, rows, s),
            "erecv": vmem(8, rows, s),
            "merged": vmem(8, 2, rows, s),
            "sums": vmem(2, NY, 2, own, 3 * s),
            "csums": vmem(NY, 2, own, 3 * s),
            "chip": vmem(NY, 2, own, 3 * s),
            "gz": vmem(NY, own, 2 * s),
            "gsum": vmem(NY, own, 2 * s),
            "gy": vmem(3, own, 2 * s),
            "ny": vmem(3, 2, own, s),
            "nsum": vmem(2, own, s),
            "nz": vmem(own, s),
            "gown": vmem(2, own, s),
            "gall": vmem(NY, 2, 2, own, s),
            "dall": vmem(8, rows, s),
        }
        for _, s in chunks
    ]
    copies = 16 + 44 * len(chunks)
    wide = max(s for _, s in chunks)
    whole = pl.BlockSpec(memory_space=pltpu.VMEM)
    node, agrad, egrad = pl.pallas_call(
        functools.partial(kernel, chunks),
        out_shape=(
            jax.ShapeDtypeStruct((own, width), BF16),
            jax.ShapeDtypeStruct((own, width), F32),
            jax.ShapeDtypeStruct((n_exp, rows, width), F32),
        ),
        in_specs=[
            whole,
            pl.BlockSpec(memory_space=pltpu.SMEM),
            whole,
            whole,
            pl.BlockSpec(memory_space=pl.ANY),
            whole,
            whole,
            whole,
            whole,
        ],
        out_specs=(whole, whole, whole),
        scratch_shapes=[
            vmem(n_edges, width),
            vmem(8, 2, own, width),
            vmem(8, 2, own, width),
            vmem(n_edges, n_atoms),
            vmem(n_edges, n_atoms),
            vmem(n_atoms, n_edges),
            vmem(n_atoms, n_edges),
            vmem(128, n_atoms),
            vmem(2, n_atoms, wide),
            vmem(n_edges, 2 * wide),
            per_chunk,
            pltpu.SemaphoreType.DMA((1,)),
            pltpu.SemaphoreType.DMA((copies,)),
            pltpu.SemaphoreType.DMA((copies,)),
        ],
        compiler_params=pltpu.CompilerParams(
            collective_id=0, has_side_effects=True, vmem_limit_bytes=67043328
        ),
    )(
        experts,
        coef,
        atoms[0],
        cotangent[0],
        radial[0],
        source.reshape(n_edges // 128, 128),
        target.reshape(n_edges // 128, 128),
        source,
        target,
    )
    return node[None], agrad[None], egrad


def solution(mesh):
    spec = P("sys", "edge", None)
    return jax.shard_map(
        layer,
        mesh=mesh,
        in_specs=(spec, spec, spec, spec, P(), P("sys", "edge"), P("sys", "edge")),
        out_specs=(spec, spec, spec),
        check_vma=False,
    )
```

time: 370 us -> 150 us (0.41)
  waiting for transfers between devices: 164 us -> 0 us
  Pallas kernels: 0 us -> 143 us
  other arithmetic: 77.5 us -> 0 us
  local copies, waits for them, and re-layouts: 55.9 us -> 5.87 us
  matrix products: 44.9 us -> 0 us
  between operations: 15.8 us -> 0.64 us
  blocking collectives: 11.2 us -> 0 us
    reduce_scatter x3 -> x0, waiting for transfers between devices: 163 us -> none  [the longest x1 85.3 us: shards(): lax.psum_scatter(jnp.einsum('se,erd->srd', chosen, own_experts, precision...]
    pallas_call x0 -> x1, Pallas kernels: none -> 143 us  [layer(): pl.pallas_call(functools.partial(kernel, chunks), out_shape=(jax.ShapeDty...]
    scatter-add x3 -> x0, other arithmetic: 62.2 us -> none  [the longest x1 22.2 us: shards(): jax.ops.segment_sum(message.astype(jnp.float32), tgt_idx, num_segments=at...]
    dot_general x5 -> x0, matrix products: 44.9 us -> none  [the longest x1 15.8 us: shards(): pre = jnp.dot(edge_in, full_weight, preferred_element_type=jnp.float32)]
    gather x3 -> x0, local copies, waits for them, and re-layouts: 31.3 us -> none  [the longest x1 12.3 us: shards(): edge_cot = jnp.take(all_cot, tgt_idx, axis=0).astype(jnp.float32)]
    all_gather x1 -> x0, blocking collectives: 11.2 us -> none  [gather_in_order(): parts = lax.all_gather(parts, axes[k])]
    all_gather x1 -> x0, local copies, waits for them, and re-layouts: 5.64 us -> none  [gather_in_order(): parts = lax.all_gather(parts, axes[k])]
    select_n x1 -> x0, other arithmetic: 5.61 us -> none  [shards(): jnp.take(all_atoms, tgt_idx, axis=0)]
  transfers between devices with their start and end apart: 6 -> 0, of which waited for: 2 -> 0; matrix products, arithmetic and copies ran while one was open for 35% -> 0% of each run, Pallas kernels for 0% -> 0%
where the time goes in v1:
time: 150 us
  Pallas kernels  143 us (95%)
  local copies, waits for them, and re-layouts  5.87 us (4%)
    pallas_call x1, Pallas kernels, layer(): pl.pallas_call(functools.partial(kernel, chunks), out_shape=(jax.ShapeDty...  143 us
    unnamed x3, local copies, waits for them, and re-layouts  5.87 us

profile of v1, /device:TPU:1, one launch (start us, length us, event | category | flops | bytes accessed | tf_op | source)
XLA Modules:
  0.0 149.8 jit_solution(14980675484179255548)
XLA Ops:
  0.6 143.3 %shard_map.94 = (bf16[64,896]{1,0:T(8,128)(2,1)}, f32[64,896]{1,0:T(8,128)}, f32[4,112,896]{2,1,0:T(8,128)}) custom-call(bf16[4,112,896]{2,1,0:T(8,128)(2,1)} %experts.1, f32[8,32]{1,0:T(8,128)} %coef.1, bf16[64,896]{1,0:T(8,128)(2,1)} %bitcast.10, bf16[64,896]{1,0:T(8,128)(2,1)} %bitcast.11, bf16[2048,896]{1,0:T(8,128)(2,1)} %bitcast.7, ...), custom_call_target="tpu_custom_call" | custom-call | tf_op jit(solution)/shard_map/pallas_call | solution.py:409
  143.9 1.6 %copy.13 = bf16[1,64,896]{2,1,0:T(8,128)(2,1)} copy(bf16[1,64,896]{2,1,0:T(8,128)(2,1)} %bitcast.9) | data formatting | bytes 229376
  145.5 1.6 %copy.14 = f32[1,64,896]{2,1,0:T(8,128)} copy(f32[1,64,896]{2,1,0:T(8,128)} %bitcast.8) | data formatting | bytes 458752
  147.1 2.7 %copy.15 = f32[4,112,896]{2,1,0:T(8,128)} copy(f32[4,112,896]{2,1,0:T(8,128)} %get-tuple-element.14) | data formatting | bytes 3211264

commit v2 on v1

--- a/solution.py
+++ b/solution.py
@@ -13,6 +13,7 @@
 NX, NY = 4, 4
 SHIFTS = (2, 1, 3)
 SYS_STEPS = tuple((dz, dx) for dx in (2, 1, 3, 0) for dz in (1, 0) if (dz, dx) != (0, 0))
+EDGE_STEPS = tuple((dy, dz) for dy in (2, 1, 3, 0) for dz in (1, 0) if (dy, dz) != (0, 0))
 
 
 def dot(a, b):
@@ -25,10 +26,10 @@
 
 def kernel(
     chunks,
-    experts,
+    experts_hbm,
     coef,
-    atoms,
-    cot,
+    atoms_hbm,
+    cot_hbm,
     radial_hbm,
     src_rows,
     tgt_rows,
@@ -37,9 +38,9 @@
     node_out,
     atom_grad,
     expert_grad,
+    experts,
     radial,
     at_all,
-    ct_all,
     oh_src,
     oh_tgt,
     ot_src,
@@ -53,10 +54,11 @@
     recv_sem,
 ):
     n_exp, rows, width = experts.shape
-    own_atoms = atoms.shape[0]
+    own_atoms = atoms_hbm.shape[0]
     n_atoms = 16 * own_atoms
     n_edges = radial.shape[0]
-    n_sys = 2 * NX
+    n = len(chunks)
+    last = n - 1
     sys_id = lax.axis_index("sys")
     edge_id = lax.axis_index("edge")
     zh, x = sys_id // NX, sys_id % NX
@@ -66,17 +68,33 @@
     def sys_peer(dz, dx):
         return (((zh + dz) % 2) * NX + (x + dx) % NX, edge_id)
 
+    def edge_peer(dy, dz):
+        return (sys_id, ((y + dy) % NY) * 4 + ((zl + dz) % 2) * 2 + c)
+
     def y_peer(d):
-        return (sys_id, ((y + d) % NY) * 4 + zl * 2 + c)
-
-    z_peer = (sys_id, y * 4 + (1 - zl) * 2 + c)
+        return edge_peer(d, 0)
+
+    z_peer = edge_peer(0, 1)
     c_peer = (sys_id, y * 4 + zl * 2 + (1 - c))
 
-    radial_copy = pltpu.make_async_copy(radial_hbm, radial, local_sem.at[0])
-    radial_copy.start()
+    inputs = []
+
+    def fetch(src, dst):
+        cp = pltpu.make_async_copy(src, dst, local_sem.at[len(inputs)])
+        cp.start()
+        inputs.append(cp)
+        return cp
+
+    atoms_in = fetch(atoms_hbm, at_all.at[plane, c])
+    cot_in = [
+        fetch(cot_hbm.at[:, start : start + size], per_chunk[k]["cots"].at[plane, c])
+        for k, (start, size) in enumerate(chunks)
+    ]
+    experts_in = fetch(experts_hbm, experts)
+    radial_in = fetch(radial_hbm, radial)
 
     barrier = pltpu.get_barrier_semaphore()
-    peers = [sys_peer(dz, dx) for dz, dx in SYS_STEPS] + [y_peer(d) for d in SHIFTS] + [z_peer, c_peer]
+    peers = [sys_peer(dz, dx) for dz, dx in SYS_STEPS] + [edge_peer(dy, dz) for dy, dz in EDGE_STEPS] + [c_peer]
     for p in peers:
         pl.semaphore_signal(barrier, inc=1, device_id=p, device_id_type=MESH)
     pl.semaphore_wait(barrier, len(peers))
@@ -97,51 +115,70 @@
         sent.append(cp)
         return cp
 
-    at_all[pl.ds(plane, 1), pl.ds(c, 1)] = atoms[...][None, None]
-    ct_all[pl.ds(plane, 1), pl.ds(c, 1)] = cot[...][None, None]
-    pairs = ((atoms, at_all), (cot, ct_all))
-    a_z = [send(own, full.at[plane, c], z_peer) for own, full in pairs]
-    a_y = [send(own, full.at[plane, c], y_peer(d)) for own, full in pairs for d in SHIFTS]
-
-    e_recv = [None] * len(chunks)
+    def share(full):
+        own = full.at[plane, c]
+        return {"full": full, "z": send(own, own, z_peer), "y": [send(own, own, y_peer(d)) for d in SHIFTS]}
+
+    def share_forward(m):
+        m["z"].wait_recv()
+        other = m["full"].at[y * 2 + 1 - zl, c]
+        m["y"] += [send(other, other, y_peer(d)) for d in SHIFTS]
+
+    def share_core(m):
+        for cp in m["y"]:
+            cp.wait_recv()
+        half = m["full"].at[:, c]
+        m["c"] = send(half, half, c_peer)
+
+    def share_wait(m):
+        m["c"].wait_recv()
+
+    e_x, e_z, merged_at, cots_at = ([None] * n for _ in range(4))
 
     def expert_part(k):
         start, size = chunks[k]
         b = per_chunk[k]
-        e_recv[k] = []
-        for i, (dz, dx) in enumerate(SYS_STEPS + ((0, 0),)):
-            to = ((zh + dz) % 2) * NX + (x + dx) % NX
-            total = jnp.zeros((rows, size), F32)
-            for e in range(n_exp):
-                total += coef[to, sys_id * n_exp + e] * experts[e, :, start : start + size].astype(F32)
-            b["epart"][i] = total.astype(BF16)
-            if (dz, dx) != (0, 0):
-                e_recv[k].append(send(b["epart"].at[i], b["erecv"].at[i], sys_peer(dz, dx)))
-
-    m_z, m_y, m_f = ([None] * len(chunks) for _ in range(3))
+        for i, dx in enumerate(SHIFTS + (0,)):
+            for z in range(2):
+                to = z * NX + (x + dx) % NX
+                total = jnp.zeros((rows, size), F32)
+                for e in range(n_exp):
+                    total += coef[to, sys_id * n_exp + e] * experts[e, :, start : start + size].astype(F32)
+                b["epart"][i, z] = total.astype(BF16)
+        e_x[k] = [send(b["epart"].at[i], b["erecv"].at[i], sys_peer(0, dx)) for i, dx in enumerate(SHIFTS)]
+
+    def expert_x(k):
+        b = per_chunk[k]
+        for cp in e_x[k]:
+            cp.wait_recv()
+        total = b["epart"][3].astype(F32)
+        for i in range(3):
+            total += b["erecv"][i].astype(F32)
+        b["esum"][...] = total.astype(BF16)
+        e_z[k] = send(b["esum"].at[1 - zh], b["ez"], sys_peer(1, 0))
 
     def merge(k):
         b = per_chunk[k]
-        for cp in e_recv[k]:
-            cp.wait_recv()
-        total = b["epart"][n_sys - 1].astype(F32)
-        for i in range(n_sys - 1):
-            total += b["erecv"][i].astype(F32)
+        e_z[k].wait_recv()
+        total = b["esum"][pl.ds(zh, 1)][0].astype(F32) + b["ez"][...].astype(F32)
         b["merged"][pl.ds(plane, 1), pl.ds(c, 1)] = total.astype(BF16)[None, None]
-        own = b["merged"].at[plane, c]
-        m_z[k] = send(own, own, z_peer)
-        m_y[k] = [send(own, own, y_peer(d)) for d in SHIFTS]
+        merged_at[k] = share(b["merged"])
+        if k > 0:
+            cots_at[k] = share(b["cots"])
 
     def merge_forward(k):
-        m_z[k].wait_recv()
-        other = per_chunk[k]["merged"].at[y * 2 + 1 - zl, c]
-        m_f[k] = [send(other, other, y_peer(d)) for d in SHIFTS]
-
-    def merge_finish(k):
-        for cp in m_y[k] + m_f[k]:
-            cp.wait_recv()
-        half = per_chunk[k]["merged"].at[:, c]
-        send(half, half, c_peer).wait_recv()
+        share_forward(merged_at[k])
+        if k > 0:
+            share_forward(cots_at[k])
+
+    def merge_core(k):
+        share_core(merged_at[k])
+        if k > 0:
+            share_core(cots_at[k])
+
+    def merge_wait(k):
+        share_wait(merged_at[k])
+        share_wait(cots_at[k])
 
     def one_hots():
         lane = lax.broadcasted_iota(jnp.int32, (128, 128), 1)
@@ -192,7 +229,7 @@
             at = pl.ds(pl.multiple_of(t * 512, 512), 512)
             o_s, o_t = oh_src[at, :], oh_tgt[at, :]
             pre = dot(o_s, proj[0, :, 0:size]) + dot(o_t, proj[1, :, 0:size])
-            edge_cot = dot(o_t, ct_all[:, :, :, cols].reshape(n_atoms, size))
+            edge_cot = dot(o_t, b["cots"][...].reshape(n_atoms, size))
             r = radial[at, cols].astype(F32)
             g = 1.0 / (1.0 + jnp.exp(-pre))
             edge_vals[at, 0:size] = (edge_cot * r * (g * (1.0 + pre * (1.0 - g)))).astype(BF16)
@@ -201,7 +238,7 @@
 
         lax.fori_loop(0, n_edges // 512, pick, 0)
 
-    c_recv = [None] * len(chunks)
+    c_recv = [None] * n
 
     def sums(k):
         size = chunks[k][1]
@@ -220,7 +257,7 @@
                 b["sums"][(*spot, slice(None), slice(size, 3 * size))] = by_tgt[r][None, None, None]
             c_recv[k].append((d, send(b["sums"].at[1 - c, yy], b["csums"].at[yy], c_peer)))
 
-    g_z, n_y, g_y, n_z, q_y, q_z, q_c, d_s = ([None] * len(chunks) for _ in range(8))
+    g_z, n_y, g_y, n_z, q_y, q_z, q_c, d_z, d_x = ([None] * n for _ in range(9))
 
     def reduce_core(k):
         size = chunks[k][1]
@@ -230,36 +267,48 @@
             yy = pl.ds((y + d) % NY, 1)
             both = b["sums"][pl.ds(c, 1), yy][0].astype(F32) + b["csums"][yy].astype(F32)
             b["chip"][yy] = both.astype(BF16)
-        g_z[k] = send(b["chip"].at[:, 1 - zl, :, 0 : 2 * size], b["gz"], z_peer)
+        if k == last:
+            g_y[k] = [
+                send(b["chip"].at[(y + dy) % NY, (zl + dz) % 2, :, 0 : 2 * size], b["gd"].at[i], edge_peer(dy, dz))
+                for i, (dy, dz) in enumerate(EDGE_STEPS)
+            ]
+        else:
+            g_z[k] = send(b["chip"].at[:, 1 - zl, :, 0 : 2 * size], b["gz"], z_peer)
         n_y[k] = [
             send(b["chip"].at[(y + d) % NY, :, :, 2 * size : 3 * size], b["ny"].at[i], y_peer(d))
             for i, d in enumerate(SHIFTS)
         ]
 
     def reduce_z(k):
+        if k == last:
+            return
         size = chunks[k][1]
         b = per_chunk[k]
         g_z[k].wait_recv()
         own = b["chip"][:, pl.ds(zl, 1), :, 0 : 2 * size].reshape(NY, own_atoms, 2 * size)
         b["gsum"][...] = (own.astype(F32) + b["gz"][...].astype(F32)).astype(BF16)
         g_y[k] = [
-            send(b["gsum"].at[(y + d) % NY], b["gy"].at[i], y_peer(d)) for i, d in enumerate(SHIFTS)
+            send(b["gsum"].at[(y + d) % NY], b["gd"].at[i], y_peer(d)) for i, d in enumerate(SHIFTS)
         ]
 
     def reduce_y(k):
-        start, size = chunks[k]
+        size = chunks[k][1]
         b = per_chunk[k]
         for cp in g_y[k]:
             cp.wait_recv()
-        total = b["gsum"][pl.ds(y, 1)][0].astype(F32)
-        for i in range(3):
-            total += b["gy"][i].astype(F32)
+        if k == last:
+            total = b["chip"][pl.ds(y, 1), pl.ds(zl, 1), :, 0 : 2 * size][0, 0].astype(F32)
+        else:
+            total = b["gsum"][pl.ds(y, 1)][0].astype(F32)
+        for i in range(len(g_y[k])):
+            total += b["gd"][i].astype(F32)
         g = total.astype(BF16)
         b["gown"][0] = g[:, 0:size]
         b["gown"][1] = g[:, size : 2 * size]
         b["gall"][pl.ds(y, 1), pl.ds(zl, 1), pl.ds(c, 1)] = b["gown"][pl.ds(y // 2, 1)][None, None]
+        steps = EDGE_STEPS if k == last else tuple((d, 0) for d in SHIFTS)
         q_y[k] = [
-            send(b["gown"].at[((y + d) % NY) // 2], b["gall"].at[y, zl, c], y_peer(d)) for d in SHIFTS
+            send(b["gown"].at[((y + dy) % NY) // 2], b["gall"].at[y, zl, c], edge_peer(dy, dz)) for dy, dz in steps
         ]
         grad = dot_t(g[:, 0:size], b["merged"][0:4].reshape(width, size))
         grad += dot_t(g[:, size : 2 * size], b["merged"][4:8].reshape(width, size))
@@ -286,14 +335,17 @@
         total = b["nsum"][pl.ds(zl, 1)][0].astype(F32) + b["nz"][...].astype(F32)
         node_out[:, start : start + size] = total.astype(BF16)
 
-    def share_z(k):
+    def grad_z(k):
+        if k == last:
+            return
         for cp in q_y[k]:
             cp.wait_recv()
         part = per_chunk[k]["gall"].at[:, zl, c]
         q_z[k] = send(part, part, z_peer)
 
-    def share_c(k):
-        q_z[k].wait_recv()
+    def grad_core(k):
+        for cp in q_y[k] if k == last else [q_z[k]]:
+            cp.wait_recv()
         part = per_chunk[k]["gall"].at[:, :, c]
         q_c[k] = send(part, part, c_peer)
 
@@ -304,67 +356,100 @@
         grad = dot(sel_atoms[...], b["gall"][...].reshape(n_atoms, size))
         b["dall"][pl.ds(sys_id, 1)] = grad[0:rows].astype(BF16)[None]
         own = b["dall"].at[sys_id]
-        d_s[k] = [send(own, own, sys_peer(dz, dx)) for dz, dx in SYS_STEPS]
+        if k == last:
+            d_x[k] = [send(own, own, sys_peer(dz, dx)) for dz, dx in SYS_STEPS]
+        else:
+            d_z[k] = send(own, own, sys_peer(1, 0))
+            d_x[k] = [send(own, own, sys_peer(0, dx)) for dx in SHIFTS]
+
+    def expert_forward(k):
+        if k == last:
+            return
+        d_z[k].wait_recv()
+        other = per_chunk[k]["dall"].at[(1 - zh) * NX + x]
+        d_x[k] += [send(other, other, sys_peer(0, dx)) for dx in SHIFTS]
 
     def expert_finish(k):
         start, size = chunks[k]
         b = per_chunk[k]
-        for cp in d_s[k]:
+        for cp in d_x[k]:
             cp.wait_recv()
         for e in range(n_exp):
             total = jnp.zeros((rows, size), F32)
-            for s in range(n_sys):
+            for s in range(2 * NX):
                 total += coef[s, sys_id * n_exp + e] * b["dall"][s].astype(F32)
             expert_grad[e, :, start : start + size] = total
 
-    n = len(chunks)
+    atoms_in.wait()
+    atoms_at = share(at_all)
+    for cp in cot_in:
+        cp.wait()
+    cots_at[0] = share(per_chunk[0]["cots"])
+    experts_in.wait()
     for k in range(n):
         expert_part(k)
     one_hots()
-    for cp in a_z:
-        cp.wait_recv()
-    other = y * 2 + 1 - zl
-    a_f = [send(full.at[other, c], full.at[other, c], y_peer(d)) for _, full in pairs for d in SHIFTS]
+    share_forward(atoms_at)
+    share_forward(cots_at[0])
+    expert_x(0)
     merge(0)
+    expert_x(1)
     merge_forward(0)
-    for cp in a_y + a_f:
-        cp.wait_recv()
-    a_c = [send(full.at[:, c], full.at[:, c], c_peer) for _, full in pairs]
-    if n > 1:
-        merge(1)
-    for cp in a_c:
-        cp.wait_recv()
+    share_core(atoms_at)
+    share_core(cots_at[0])
+    merge(1)
+    merge_core(0)
+    share_wait(atoms_at)
     select_atoms()
-    radial_copy.wait()
-    if n > 1:
-        merge_forward(1)
-    merge_finish(0)
-
-    def steps(k, half):
-        if half == 0:
-            todo = [(merge, k + 2), (reduce_z, k - 1), (share_z, k - 2), (expert_finish, k - 3)]
-        else:
-            todo = [
+    radial_in.wait()
+    expert_x(2)
+    merge_forward(1)
+    merge_wait(0)
+
+    def run(todo):
+        for f, i in todo:
+            if 0 <= i < n:
+                f(i)
+
+    for k in range(n):
+        edges(k)
+        run(
+            [
+                (merge_core, k + 1),
+                (merge, k + 2),
+                (expert_x, k + 3),
+                (reduce_z, k - 1),
+                (grad_z, k - 2),
+                (expert_forward, k - 3),
+            ]
+        )
+        sums(k)
+        run(
+            [
                 (reduce_core, k),
                 (merge_forward, k + 2),
-                (merge_finish, k + 1),
+                (merge_wait, k + 1),
                 (reduce_y, k - 1),
                 (node_z, k - 1),
-                (share_c, k - 2),
+                (grad_core, k - 2),
                 (weight_grad, k - 2),
                 (node_finish, k - 2),
             ]
-        for f, i in todo:
-            if 0 <= i < n:
-                f(i)
-
-    for k in range(n + 3):
-        if k < n:
-            edges(k)
-        steps(k, 0)
-        if k < n:
-            sums(k)
-        steps(k, 1)
+        )
+    run(
+        [
+            (grad_z, n - 2),
+            (reduce_y, n - 1),
+            (expert_forward, n - 3),
+            (grad_core, n - 2),
+            (weight_grad, n - 2),
+            (node_z, n - 1),
+            (grad_core, n - 1),
+            (weight_grad, n - 1),
+            (expert_forward, n - 2),
+        ]
+    )
+    run([(node_finish, n - 2), (node_finish, n - 1)] + [(expert_finish, k) for k in range(n)])
     for cp in sent:
         cp.wait_send()
 
@@ -385,15 +470,18 @@
 
     per_chunk = [
         {
-            "epart": vmem(8, rows, s),
-            "erecv": vmem(8, rows, s),
+            "epart": vmem(4, 2, rows, s),
+            "erecv": vmem(3, 2, rows, s),
+            "esum": vmem(2, rows, s),
+            "ez": vmem(rows, s),
+            "cots": vmem(8, 2, own, s),
             "merged": vmem(8, 2, rows, s),
             "sums": vmem(2, NY, 2, own, 3 * s),
             "csums": vmem(NY, 2, own, 3 * s),
             "chip": vmem(NY, 2, own, 3 * s),
             "gz": vmem(NY, own, 2 * s),
             "gsum": vmem(NY, own, 2 * s),
-            "gy": vmem(3, own, 2 * s),
+            "gd": vmem(7, own, 2 * s),
             "ny": vmem(3, 2, own, s),
             "nsum": vmem(2, own, s),
             "nz": vmem(own, s),
@@ -403,9 +491,10 @@
         }
         for _, s in chunks
     ]
-    copies = 16 + 44 * len(chunks)
+    copies = 8 + 54 * len(chunks)
     wide = max(s for _, s in chunks)
     whole = pl.BlockSpec(memory_space=pltpu.VMEM)
+    hbm = pl.BlockSpec(memory_space=pl.ANY)
     node, agrad, egrad = pl.pallas_call(
         functools.partial(kernel, chunks),
         out_shape=(
@@ -414,11 +503,11 @@
             jax.ShapeDtypeStruct((n_exp, rows, width), F32),
         ),
         in_specs=[
-            whole,
+            hbm,
             pl.BlockSpec(memory_space=pltpu.SMEM),
-            whole,
-            whole,
-            pl.BlockSpec(memory_space=pl.ANY),
+            hbm,
+            hbm,
+            hbm,
             whole,
             whole,
             whole,
@@ -426,8 +515,8 @@
         ],
         out_specs=(whole, whole, whole),
         scratch_shapes=[
+            vmem(n_exp, rows, width),
             vmem(n_edges, width),
-            vmem(8, 2, own, width),
             vmem(8, 2, own, width),
             vmem(n_edges, n_atoms),
             vmem(n_edges, n_atoms),
@@ -437,7 +526,7 @@
             vmem(2, n_atoms, wide),
             vmem(n_edges, 2 * wide),
             per_chunk,
-            pltpu.SemaphoreType.DMA((1,)),
+            pltpu.SemaphoreType.DMA((3 + len(chunks),)),
             pltpu.SemaphoreType.DMA((copies,)),
             pltpu.SemaphoreType.DMA((copies,)),
         ],

time: 150 us -> 126 us (0.84)
  Pallas kernels: 143 us -> 120 us
    pallas_call x1, Pallas kernels: 143 us -> 120 us  [layer(): pl.pallas_call(functools.partial(kernel, chunks), out_shape=(jax.ShapeDty...]
where the time goes in v2:
time: 126 us
  Pallas kernels  120 us (95%)
  local copies, waits for them, and re-layouts  5.87 us (5%)
    pallas_call x1, Pallas kernels, layer(): pl.pallas_call(functools.partial(kernel, chunks), out_shape=(jax.ShapeDty...  120 us
    unnamed x3, local copies, waits for them, and re-layouts  5.87 us

profile of v2, /device:TPU:1, one launch (start us, length us, event | category | flops | bytes accessed | tf_op | source)
XLA Modules:
  0.0 126.0 jit_solution(3630655268326168132)
XLA Ops:
  0.6 119.5 %shard_map.94 = (bf16[64,896]{1,0:T(8,128)(2,1)}, f32[64,896]{1,0:T(8,128)}, f32[4,112,896]{2,1,0:T(8,128)}) custom-call(bf16[4,112,896]{2,1,0:T(8,128)(2,1)} %experts_hbm.1, f32[8,32]{1,0:T(8,128)} %coef.1, bf16[64,896]{1,0:T(8,128)(2,1)} %bitcast.10, bf16[64,896]{1,0:T(8,128)(2,1)} %bitcast.11, bf16[2048,896]{1,0:T(8,128)(2,1)} %bitcast.7, ...), custom_call_target="tpu_custom_call" | custom-call | tf_op jit(solution)/shard_map/pallas_call | solution.py:498
  120.2 1.6 %copy.13 = bf16[1,64,896]{2,1,0:T(8,128)(2,1)} copy(bf16[1,64,896]{2,1,0:T(8,128)(2,1)} %bitcast.9) | data formatting | bytes 229376
  121.7 1.6 %copy.14 = f32[1,64,896]{2,1,0:T(8,128)} copy(f32[1,64,896]{2,1,0:T(8,128)} %bitcast.8) | data formatting | bytes 458752
  123.4 2.7 %copy.15 = f32[4,112,896]{2,1,0:T(8,128)} copy(f32[4,112,896]{2,1,0:T(8,128)} %get-tuple-element.14) | data formatting | bytes 3211264

commit v3 on v2

v3 whole, which is shorter than its diff:
```python
import functools

import jax
import jax.numpy as jnp
from jax import lax
from jax.experimental import pallas as pl
from jax.experimental.pallas import tpu as pltpu
from jax.sharding import PartitionSpec as P

F32 = jnp.float32
BF16 = jnp.bfloat16
MESH = pl.DeviceIdType.MESH
NX, NY = 4, 4
SHIFTS = (2, 1, 3)
SEND_SLOTS = 64
RECV_SLOTS = 200
SYS_STEPS = tuple((dz, dx) for dx in (2, 1, 3, 0) for dz in (1, 0) if (dz, dx) != (0, 0))
EDGE_STEPS = tuple((dy, dz) for dy in (2, 1, 3, 0) for dz in (1, 0) if (dy, dz) != (0, 0))


def dot(a, b):
    return lax.dot_general(a, b, (((1,), (0,)), ((), ())), preferred_element_type=F32)


def dot_t(a, b):
    return lax.dot_general(a, b, (((1,), (1,)), ((), ())), preferred_element_type=F32)


def kernel(
    chunks,
    experts_hbm,
    coef,
    atoms_hbm,
    cot_hbm,
    radial_hbm,
    src_rows,
    tgt_rows,
    src_line,
    tgt_line,
    node_hbm,
    atom_hbm,
    expert_hbm,
    node_out,
    atom_grad,
    expert_grad,
    atom_total,
    atom_send,
    atom_z,
    atom_d,
    experts,
    radial,
    at_all,
    oh_src,
    oh_tgt,
    ot_src,
    ot_tgt,
    sel_atoms,
    proj,
    edge_vals,
    per_chunk,
    local_sem,
    send_sem,
    recv_sem,
):
    n_exp, rows, width = experts.shape
    own_atoms = atoms_hbm.shape[0]
    n_atoms = 16 * own_atoms
    n_edges = radial.shape[0]
    n = len(chunks)
    direct = n - 2
    sys_id = lax.axis_index("sys")
    edge_id = lax.axis_index("edge")
    zh, x = sys_id // NX, sys_id % NX
    y, zl, c = edge_id // 4, (edge_id // 2) % 2, edge_id % 2

    def sys_peer(dz, dx):
        return (((zh + dz) % 2) * NX + (x + dx) % NX, edge_id)

    def edge_peer(dy, dz):
        return (sys_id, ((y + dy) % NY) * 4 + ((zl + dz) % 2) * 2 + c)

    def y_peer(d):
        return edge_peer(d, 0)

    z_peer = edge_peer(0, 1)
    c_peer = (sys_id, y * 4 + zl * 2 + (1 - c))

    inputs = []

    def fetch(src, dst):
        cp = pltpu.make_async_copy(src, dst, local_sem.at[len(inputs)])
        cp.start()
        inputs.append(cp)
        return cp

    atoms_in = fetch(atoms_hbm, at_all.at[y, zl, c])
    cot_in = [
        fetch(cot_hbm.at[:, start : start + size], per_chunk[k]["cots"].at[y, zl, c])
        for k, (start, size) in enumerate(chunks)
    ]
    experts_in = fetch(experts_hbm, experts)
    radial_in = fetch(radial_hbm, radial)

    barrier = pltpu.get_barrier_semaphore()
    peers = [sys_peer(dz, dx) for dz, dx in SYS_STEPS] + [edge_peer(dy, dz) for dy, dz in EDGE_STEPS] + [c_peer]
    for p in peers:
        pl.semaphore_signal(barrier, inc=1, device_id=p, device_id_type=MESH)
    pl.semaphore_wait(barrier, len(peers))

    sent = []

    def send(src, dst, peer):
        i = len(sent)
        if i >= SEND_SLOTS:
            sent[i - SEND_SLOTS].wait_send()
        cp = pltpu.make_async_remote_copy(
            src_ref=src,
            dst_ref=dst,
            send_sem=send_sem.at[i % SEND_SLOTS],
            recv_sem=recv_sem.at[i],
            device_id=peer,
            device_id_type=MESH,
        )
        cp.start()
        sent.append(cp)
        return cp

    def share(full, cut):
        lo = full.at[:, :, :, 0:cut]
        own = lo.at[y, zl, c]
        m = {"full": full, "lo": lo, "y": []}
        if cut < full.shape[3]:
            m["hi"] = full.at[:, :, :, cut : full.shape[3]]
            block = m["hi"].at[y, zl, c]
            m["yh"] = [send(block, block, y_peer(d)) for d in SHIFTS]
        m["z"] = send(own, own, z_peer)
        m["y"] += [send(own, own, y_peer(d)) for d in SHIFTS]
        return m

    def share_forward(m):
        m["z"].wait_recv()
        other = m["lo"].at[y, 1 - zl, c]
        m["y"] += [send(other, other, y_peer(d)) for d in SHIFTS]

    def share_across(m):
        for cp in m["yh"]:
            cp.wait_recv()
        column = m["hi"].at[:, zl, c]
        m["y"].append(send(column, column, z_peer))

    def share_core(m):
        for cp in m["y"]:
            cp.wait_recv()
        half = m["full"].at[:, :, c]
        m["c"] = send(half, half, c_peer)

    def share_wait(m):
        m["c"].wait_recv()

    e_x, e_z, merged_at, cots_at = ([None] * n for _ in range(4))

    def expert_part(k):
        start, size = chunks[k]
        b = per_chunk[k]
        for i, dx in enumerate(SHIFTS + (0,)):
            for z in range(2):
                to = z * NX + (x + dx) % NX
                total = jnp.zeros((rows, size), F32)
                for e in range(n_exp):
                    total += coef[to, sys_id * n_exp + e] * experts[e, :, start : start + size].astype(F32)
                b["epart"][i, z] = total.astype(BF16)
        if k == 0:
            e_z[0] = [
                send(b["epart"].at[(SHIFTS + (0,)).index(dx), (zh + dz) % 2], b["ez"].at[i], sys_peer(dz, dx))
                for i, (dz, dx) in enumerate(SYS_STEPS)
            ]
        else:
            e_x[k] = [send(b["epart"].at[i], b["erecv"].at[i], sys_peer(0, dx)) for i, dx in enumerate(SHIFTS)]

    def expert_x(k):
        b = per_chunk[k]
        for cp in e_x[k]:
            cp.wait_recv()
        total = b["epart"][3].astype(F32)
        for i in range(3):
            total += b["erecv"][i].astype(F32)
        b["esum"][...] = total.astype(BF16)
        e_z[k] = [send(b["esum"].at[1 - zh], b["ez"].at[0], sys_peer(1, 0))]

    def merge(k):
        b = per_chunk[k]
        for cp in e_z[k]:
            cp.wait_recv()
        own = b["epart"].at[3] if k == 0 else b["esum"]
        total = own[pl.ds(zh, 1)][0].astype(F32)
        for i in range(len(e_z[k])):
            total += b["ez"][i].astype(F32)
        b["merged"][pl.ds(y, 1), pl.ds(zl, 1), pl.ds(c, 1)] = total.astype(BF16)[None, None, None]
        merged_at[k] = share(b["merged"], 48 if k == 0 else rows)
        if k > 0:
            cots_at[k] = share(b["cots"], own_atoms)

    def merge_forward(k):
        share_forward(merged_at[k])
        if k > 0:
            share_forward(cots_at[k])

    def merge_core(k):
        share_core(merged_at[k])
        if k > 0:
            share_core(cots_at[k])

    def merge_wait(k):
        share_wait(merged_at[k])
        share_wait(cots_at[k])

    def one_hots():
        lane = lax.broadcasted_iota(jnp.int32, (128, 128), 1)

        def by_edge(j, _):
            at = pl.ds(pl.multiple_of(j * 128, 128), 128)
            for idx, out in ((src_rows, oh_src), (tgt_rows, oh_tgt)):
                col = jnp.broadcast_to(idx[pl.ds(j, 1), :], (128, 128)).T
                for a in range(n_atoms // 128):
                    out[at, a * 128 : (a + 1) * 128] = jnp.where(col == lane + a * 128, 1.0, 0.0).astype(BF16)
            return 0

        lax.fori_loop(0, n_edges // 128, by_edge, 0)
        sub = lax.broadcasted_iota(jnp.int32, (64, n_edges), 0)

        def by_atom(j, _):
            at = pl.ds(pl.multiple_of(j * 64, 64), 64)
            for idx, out in ((src_line, ot_src), (tgt_line, ot_tgt)):
                line = jnp.broadcast_to(idx[...], (64, n_edges)) - j * 64
                out[at, :] = jnp.where(line == sub, 1.0, 0.0).astype(BF16)
            return 0

        lax.fori_loop(0, n_atoms // 64, by_atom, 0)

    def select_atoms():
        count = 4 * rows
        i = lax.broadcasted_iota(jnp.int32, (count, width), 0)
        j = lax.broadcasted_iota(jnp.int32, (count, width), 1)
        pick = jnp.where(j == i + (i // rows + c) * rows, 1.0, 0.0).astype(BF16)
        sel_atoms[...] = dot_t(pick, at_all[...].reshape(n_atoms, width)).astype(BF16)

    def project(k):
        size = chunks[k][1]
        b = per_chunk[k]
        narrow = 2 * size <= proj.shape[2]

        def body(t, _):
            at = pl.ds(pl.multiple_of(t * 256, 256), 256)
            a = at_all[pl.ds(t, 1)].reshape(256, width)
            w = [b["merged"][2 * h : 2 * h + 2].reshape(width, size) for h in range(2)]
            if narrow:
                both = dot(a, jnp.concatenate(w, axis=1)).astype(BF16)
                proj[0, at, 0:size] = both[:, 0:size]
                proj[1, at, 0:size] = both[:, size : 2 * size]
                proj[1, at, size : 2 * size] = b["cots"][pl.ds(t, 1)].reshape(256, size)
            else:
                for h in range(2):
                    proj[h, at, 0:size] = dot(a, w[h]).astype(BF16)
            return 0

        lax.fori_loop(0, NY, body, 0)

    def pick(k, half):
        start, size = chunks[k]
        b = per_chunk[k]
        narrow = 2 * size <= proj.shape[2]
        count = n_edges // 1024

        def body(t, _):
            at = pl.ds(pl.multiple_of(t * 512, 512), 512)
            o_s, o_t = oh_src[at, :], oh_tgt[at, :]
            if narrow:
                by_tgt = dot(o_t, proj[1, :, 0 : 2 * size])
                edge_cot = by_tgt[:, size : 2 * size]
                pre = dot(o_s, proj[0, :, 0:size]) + by_tgt[:, 0:size]
            else:
                pre = dot(o_s, proj[0, :, 0:size]) + dot(o_t, proj[1, :, 0:size])
                edge_cot = dot(o_t, b["cots"][...].reshape(n_atoms, size))
            r = radial[at, start : start + size].astype(F32)
            g = 1.0 / (1.0 + jnp.exp(-pre))
            edge_vals[at, 0:size] = (edge_cot * r * (g * (1.0 + pre * (1.0 - g)))).astype(BF16)
            edge_vals[at, size : 2 * size] = (pre * g * r).astype(BF16)
            return 0

        lax.fori_loop(half * count, (half + 1) * count, body, 0)

    c_recv = [None] * n

    def sums(k, tiles):
        size = chunks[k][1]
        b = per_chunk[k]
        if c_recv[k] is None:
            c_recv[k] = []
        for d in tiles:
            yy = (y + d) % NY
            at = pl.ds(pl.multiple_of(yy * 256, 256), 256)
            o_s, o_t = ot_src[at, :], ot_tgt[at, :]
            by_src = dot(o_s, edge_vals[:, 0:size]).astype(BF16)
            by_tgt = dot(o_t, edge_vals[:, 0 : 2 * size]).astype(BF16)
            spot = pl.ds(yy, 1)
            b["sums"][spot, :, :, :, 0:size] = by_src.reshape(1, 2, 2, own_atoms, size)
            b["sums"][spot, :, :, :, size : 3 * size] = by_tgt.reshape(1, 2, 2, own_atoms, 2 * size)
            c_recv[k].append((d, send(b["sums"].at[yy], b["csums"].at[yy], c_peer)))

    w_z, w_y, g_z, g_y, n_y, n_z, d_z, d_x = ([None] * n for _ in range(8))
    a_yz = []

    def to_edge(block_of, landing):
        return [send(block_of(dy, dz), landing.at[i], edge_peer(dy, dz)) for i, (dy, dz) in enumerate(EDGE_STEPS)]

    def atoms_of(dy, dz):
        return (y + dy) % NY, (zl + dz) % 2

    def reduce_core(k):
        size = chunks[k][1]
        b = per_chunk[k]
        for d, cp in c_recv[k]:
            cp.wait_recv()
            spot = pl.ds((y + d) % NY, 1)
            both = b["sums"][spot, :, :, :, 0 : 2 * size].astype(F32) + b["csums"][spot, :, :, :, 0 : 2 * size].astype(F32)
            b["chip"][spot] = both.astype(BF16)
        grad = dot(sel_atoms[...], b["chip"][...].reshape(n_atoms, 2 * size)).astype(BF16)
        b["wpart"][0:2] = grad[:, 0:size].reshape(2, 2, rows, size)
        b["wpart"][2:4] = grad[:, size : 2 * size].reshape(2, 2, rows, size)
        if k >= direct:
            w_y[k] = to_edge(lambda dy, dz: b["wpart"].at[atoms_of(dy, dz)], b["wd"])
            if k < n - 1:
                g_z[k] = send(b["chip"].at[:, 1 - zl, c], b["gz"], z_peer)
        else:
            w_z[k] = send(b["wpart"].at[:, 1 - zl], b["wz"], z_peer)

    def node_core(k):
        size = chunks[k][1]
        b = per_chunk[k]
        spot = (slice(None), slice(None), pl.ds(c, 1), slice(None), slice(2 * size, 3 * size))
        both = b["sums"][spot].astype(F32) + b["csums"][spot].astype(F32)
        b["nchip"][...] = both.astype(BF16).reshape(NY, 2, own_atoms, size)
        n_y[k] = [send(b["nchip"].at[(y + d) % NY], b["ny"].at[i], y_peer(d)) for i, d in enumerate(SHIFTS)]

    def node_z(k):
        b = per_chunk[k]
        for cp in n_y[k]:
            cp.wait_recv()
        total = b["nchip"][pl.ds(y, 1)][0].astype(F32)
        for i in range(3):
            total += b["ny"][i].astype(F32)
        b["nsum"][...] = total.astype(BF16)
        n_z[k] = send(b["nsum"].at[1 - zl], b["nz"], z_peer)

    def node_finish(k):
        start, size = chunks[k]
        b = per_chunk[k]
        n_z[k].wait_recv()
        total = b["nsum"][pl.ds(zl, 1)][0].astype(F32) + b["nz"][...].astype(F32)
        node_out[:, start : start + size] = total.astype(BF16)

    def atom_part(k):
        size = chunks[k][1]
        b = per_chunk[k]
        g = b["chip"][:, :, pl.ds(c, 1)].reshape(n_atoms // 2, 2 * size)
        grad = dot_t(g[:, 0:size], b["merged"][0:2].reshape(width, size))
        grad += dot_t(g[:, size : 2 * size], b["merged"][2:4].reshape(width, size))
        grad = grad.reshape(NY, 2, own_atoms, width)
        if k == 0:
            atom_total[...] = grad
        else:
            atom_total[...] += grad
        if k == direct - 1:
            atom_send[...] = atom_total[...].astype(BF16)
            a_yz.extend(send(atom_send.at[(y + d) % NY], atom_d.at[i], y_peer(d)) for i, d in enumerate(SHIFTS))

    def atom_y():
        for cp in a_yz:
            cp.wait_recv()
        a_yz.clear()
        total = atom_total[pl.ds(y, 1)][0]
        for i in range(3):
            total += atom_d[i].astype(F32)
        atom_send[pl.ds(y, 1)] = total.astype(BF16)[None]
        a_yz.append(send(atom_send.at[y, 1 - zl], atom_z, z_peer))
        atom_total[pl.ds(y, 1)] = total[None]

    def atom_finish():
        a_yz.pop().wait_recv()
        atom_grad[...] = atom_total[pl.ds(y, 1), pl.ds(zl, 1)].reshape(own_atoms, width) + atom_z[...].astype(F32)

    def atom_direct(k):
        b = per_chunk[k]
        g_y[k] = to_edge(lambda dy, dz: b["chip"].at[(*atoms_of(dy, dz), c)], b["gd"])

    def atom_staged(k):
        size = chunks[k][1]
        b = per_chunk[k]
        g_z[k].wait_recv()
        own = b["chip"][:, pl.ds(zl, 1), pl.ds(c, 1)].reshape(NY, own_atoms, 2 * size)
        b["gsum"][...] = (own.astype(F32) + b["gz"][...].astype(F32)).astype(BF16)
        g_y[k] = [send(b["gsum"].at[(y + d) % NY], b["gd"].at[i], y_peer(d)) for i, d in enumerate(SHIFTS)]

    def atom_last(k):
        size = chunks[k][1]
        b = per_chunk[k]
        for cp in g_y[k]:
            cp.wait_recv()
        if k == n - 1:
            total = b["chip"][pl.ds(y, 1), pl.ds(zl, 1), pl.ds(c, 1)][0, 0, 0].astype(F32)
        else:
            total = b["gsum"][pl.ds(y, 1)][0].astype(F32)
        for i in range(len(g_y[k])):
            total += b["gd"][i].astype(F32)
        g = total.astype(BF16)
        grad = dot_t(g[:, 0:size], b["merged"][0:2].reshape(width, size))
        grad += dot_t(g[:, size : 2 * size], b["merged"][2:4].reshape(width, size))
        atom_grad[...] += grad

    def weight_z(k):
        size = chunks[k][1]
        b = per_chunk[k]
        w_z[k].wait_recv()
        own = b["wpart"][:, pl.ds(zl, 1)].reshape(NY, rows, size)
        b["wsum"][...] = (own.astype(F32) + b["wz"][...].astype(F32)).astype(BF16)
        w_y[k] = [send(b["wsum"].at[(y + d) % NY], b["wd"].at[i], y_peer(d)) for i, d in enumerate(SHIFTS)]

    def weight_finish(k):
        b = per_chunk[k]
        for cp in w_y[k]:
            cp.wait_recv()
        if k >= direct:
            total = b["wpart"][pl.ds(y, 1), pl.ds(zl, 1)][0].astype(F32)
        else:
            total = b["wsum"][pl.ds(y, 1)].astype(F32)
        for i in range(len(w_y[k])):
            total += b["wd"][i : i + 1].astype(F32)
        b["dall"][pl.ds(sys_id, 1)] = total.astype(BF16)
        own = b["dall"].at[sys_id]
        if k == n - 1:
            d_x[k] = [send(own, own, sys_peer(dz, dx)) for dz, dx in SYS_STEPS]
        else:
            d_z[k] = send(own, own, sys_peer(1, 0))
            d_x[k] = [send(own, own, sys_peer(0, dx)) for dx in SHIFTS]

    def expert_forward(k):
        d_z[k].wait_recv()
        other = per_chunk[k]["dall"].at[(1 - zh) * NX + x]
        d_x[k] += [send(other, other, sys_peer(0, dx)) for dx in SHIFTS]

    def expert_finish(k):
        start, size = chunks[k]
        b = per_chunk[k]
        for cp in d_x[k]:
            cp.wait_recv()
        for e in range(n_exp):
            total = jnp.zeros((rows, size), F32)
            for s in range(2 * NX):
                total += coef[s, sys_id * n_exp + e] * b["dall"][s].astype(F32)
            expert_grad[e, :, start : start + size] = total
        cols = slice(start, start + size)
        outputs.append(fetch(expert_grad.at[:, :, cols], expert_hbm.at[:, :, cols]))

    outputs = []
    atoms_in.wait()
    atoms_at = share(at_all, own_atoms // 2)
    for cp in cot_in:
        cp.wait()
    cots_at[0] = share(per_chunk[0]["cots"], own_atoms // 2)
    experts_in.wait()
    for k in range(n):
        expert_part(k)
    one_hots()
    share_forward(atoms_at)
    share_forward(cots_at[0])
    share_across(atoms_at)
    share_across(cots_at[0])
    merge(0)
    share_forward(merged_at[0])
    expert_x(1)
    share_core(atoms_at)
    share_across(merged_at[0])
    share_core(cots_at[0])
    share_wait(atoms_at)
    select_atoms()
    share_core(merged_at[0])
    radial_in.wait()
    merge_wait(0)

    work = (
        (project,),
        (lambda k: pick(k, 0),),
        (lambda k: pick(k, 1),),
        (lambda k: sums(k, SHIFTS[0:1]),),
        (lambda k: sums(k, SHIFTS[1:2]),),
        (lambda k: sums(k, SHIFTS[2:3]),),
        (lambda k: sums(k, (0,)),),
    )
    beside = {
        (0, 0): ((merge, 1), (expert_x, 2)),
        (0, 1): ((merge_forward, 1),),
        (0, 2): ((merge, 2),),
        (0, 4): ((merge_core, 1),),
        (0, 5): ((merge_forward, 2), (expert_x, 3)),
        (0, 6): ((merge_wait, 1),),
        (1, 0): ((reduce_core, 0), (node_core, 0), (atom_part, 0)),
        (1, 1): ((merge, 3),),
        (1, 2): ((merge_core, 2),),
        (1, 4): ((merge_wait, 2),),
        (1, 5): ((merge_forward, 3), (weight_z, 0)),
        (2, 0): ((reduce_core, 1), (node_core, 1), (atom_part, 1)),
        (2, 2): ((merge_core, 3), (weight_finish, 0)),
        (2, 3): ((node_z, 0),),
        (2, 4): ((merge_wait, 3),),
        (2, 5): ((weight_z, 1),),
        (2, 6): ((expert_forward, 0),),
        (3, 0): ((reduce_core, 2), (node_core, 2)),
        (3, 2): ((weight_finish, 1),),
        (3, 3): ((node_z, 1),),
    }
    for k in range(n):
        for slot, (f,) in enumerate(work):
            f(k)
            for g, i in beside.get((k, slot), ()):
                g(i)
            if (k, slot) == (3, 4):
                atom_y()
    reduce_core(3)
    node_core(3)
    expert_forward(1)
    weight_finish(2)
    atom_direct(3)
    atom_staged(2)
    expert_finish(0)
    weight_finish(3)
    expert_forward(2)
    atom_finish()
    expert_finish(1)
    atom_last(3)
    node_z(2)
    node_z(3)
    atom_last(2)
    outputs.append(fetch(atom_grad, atom_hbm))
    for k in range(n):
        node_finish(k)
    outputs.append(fetch(node_out, node_hbm))
    expert_finish(2)
    expert_finish(3)

    def finish():
        for cp in outputs:
            cp.wait()

    def drain():
        for cp in sent[-SEND_SLOTS:]:
            cp.wait_send()
        assert len(sent) == recv_sem.shape[0], len(sent)

    finish()
    drain()


def write_out(*refs):
    count = (len(refs) - 1) // 3
    sem = refs[-1]
    moves = []
    for src, dst, buf in zip(refs[:count], refs[count : 2 * count], refs[2 * count : 3 * count]):
        for i in range(src.shape[0]):
            moves.append((src.at[i], buf.at[i], dst.at[i]))
    reads = [pltpu.make_async_copy(s, b, sem.at[0, i]) for i, (s, b, _) in enumerate(moves)]
    writes = [pltpu.make_async_copy(b, d, sem.at[1, i]) for i, (_, b, d) in enumerate(moves)]
    for r in reads:
        r.start()
    for r, w in zip(reads, writes):
        r.wait()
        w.start()
    for w in writes:
        w.wait()


def layer(atoms, cotangent, experts, radial, coef, source, target):
    n_exp, rows, width = experts.shape
    own = atoms.shape[1]
    n_atoms = 16 * own
    n_edges = radial.shape[1]
    chunks, at = [], 0
    while at < width:
        size = min(256, width - at)
        chunks.append((at, size))
        at += size

    def vmem(*shape):
        return pltpu.VMEM(shape, BF16)

    per_chunk = [
        {
            "epart": vmem(4, 2, rows, s),
            "erecv": vmem(3, 2, rows, s),
            "esum": vmem(2, rows, s),
            "ez": vmem(7 if k == 0 else 1, rows, s),
            "cots": vmem(NY, 2, 2, own, s),
            "merged": vmem(NY, 2, 2, rows, s),
            "sums": vmem(NY, 2, 2, own, 3 * s),
            "csums": vmem(NY, 2, 2, own, 3 * s),
            "chip": vmem(NY, 2, 2, own, 2 * s),
            "nchip": vmem(NY, 2, own, s),
            "ny": vmem(3, 2, own, s),
            "nsum": vmem(2, own, s),
            "nz": vmem(own, s),
            "gz": vmem(NY if k == 2 else 1, own, 2 * s),
            "gsum": vmem(NY if k == 2 else 1, own, 2 * s),
            "gd": vmem(7 if k == 3 else 3, own, 2 * s),
            "wpart": vmem(NY, 2, rows, s),
            "wz": vmem(NY, rows, s),
            "wsum": vmem(NY, rows, s),
            "wd": vmem(7, rows, s),
            "dall": vmem(8, rows, s),
        }
        for k, (_, s) in enumerate(chunks)
    ]
    wide = max(s for _, s in chunks)
    whole = pl.BlockSpec(memory_space=pltpu.VMEM)
    hbm = pl.BlockSpec(memory_space=pl.ANY)
    node, agrad, egrad = pl.pallas_call(
        functools.partial(kernel, chunks),
        out_shape=(
            jax.ShapeDtypeStruct((own, width), BF16),
            jax.ShapeDtypeStruct((own, width), F32),
            jax.ShapeDtypeStruct((n_exp, rows, width), F32),
        ),
        in_specs=[
            hbm,
            pl.BlockSpec(memory_space=pltpu.SMEM),
            hbm,
            hbm,
            hbm,
            whole,
            whole,
            whole,
            whole,
        ],
        out_specs=(hbm, hbm, hbm),
        scratch_shapes=[
            vmem(own, width),
            pltpu.VMEM((own, width), F32),
            pltpu.VMEM((n_exp, rows, width), F32),
            pltpu.VMEM((NY, 2, own, width), F32),
            vmem(NY, 2, own, width),
            vmem(own, width),
            vmem(3, 2, own, width),
            vmem(n_exp, rows, width),
            vmem(n_edges, width),
            vmem(NY, 2, 2, own, width),
            vmem(n_edges, n_atoms),
            vmem(n_edges, n_atoms),
            vmem(n_atoms, n_edges),
            vmem(n_atoms, n_edges),
            vmem(4 * rows, n_atoms),
            vmem(2, n_atoms, wide),
            vmem(n_edges, 2 * wide),
            per_chunk,
            pltpu.SemaphoreType.DMA((5 + 2 * len(chunks),)),
            pltpu.SemaphoreType.DMA((SEND_SLOTS,)),
            pltpu.SemaphoreType.DMA((RECV_SLOTS,)),
        ],
        compiler_params=pltpu.CompilerParams(
            collective_id=0, has_side_effects=True, vmem_limit_bytes=67043328
        ),
    )(
        experts,
        coef,
        atoms[0],
        cotangent[0],
        radial[0],
        source.reshape(n_edges // 128, 128),
        target.reshape(n_edges // 128, 128),
        source,
        target,
    )
    results = (node[None], agrad[None], egrad)
    moves = sum(r.shape[0] for r in results)
    return pl.pallas_call(
        write_out,
        out_shape=tuple(jax.ShapeDtypeStruct(r.shape, r.dtype) for r in results),
        in_specs=[hbm] * 3,
        out_specs=(hbm,) * 3,
        scratch_shapes=[pltpu.VMEM(r.shape, r.dtype) for r in results] + [pltpu.SemaphoreType.DMA((2, moves))],
    )(*results)


def solution(mesh):
    spec = P("sys", "edge", None)
    return jax.shard_map(
        layer,
        mesh=mesh,
        in_specs=(spec, spec, spec, spec, P(), P("sys", "edge"), P("sys", "edge")),
        out_specs=(spec, spec, spec),
        check_vma=False,
    )
```

time: 126 us -> 110 us (0.87)
  Pallas kernels: 120 us -> 108 us
  local copies, waits for them, and re-layouts: 5.87 us -> 0 us
    pallas_call x1, Pallas kernels: 120 us -> 106 us  [layer(): pl.pallas_call(functools.partial(kernel, chunks), out_shape=(jax.ShapeDty...]
    unnamed x3 -> x0, local copies, waits for them, and re-layouts: 5.87 us -> none
    pallas_call x0 -> x1, Pallas kernels: none -> 2.42 us  [layer(): pl.pallas_call(write_out, out_shape=tuple((jax.ShapeDtypeStruct(r.shape,...]
where the time goes in v3:
time: 110 us; the launch traced here: 109 us
  Pallas kernels  108 us (98%)
    pallas_call x1, Pallas kernels, layer(): pl.pallas_call(functools.partial(kernel, chunks), out_shape=(jax.ShapeDty...  106 us
    pallas_call x1, Pallas kernels, layer(): pl.pallas_call(write_out, out_shape=tuple((jax.ShapeDtypeStruct(r.shape,...  2.42 us

profile of v3, /device:TPU:1, one launch (start us, length us, event | category | flops | bytes accessed | tf_op | source)
XLA Modules:
  0.0 109.3 jit_solution(15287938282917732880)
XLA Ops:
  0.6 106.1 %shard_map.94 = (bf16[64,896]{1,0:T(8,128)(2,1)}, f32[64,896]{1,0:T(8,128)}, f32[4,112,896]{2,1,0:T(8,128)}) custom-call(bf16[4,112,896]{2,1,0:T(8,128)(2,1)} %experts_hbm.1, f32[8,32]{1,0:T(8,128)} %coef.1, bf16[64,896]{1,0:T(8,128)(2,1)} %bitcast.9, bf16[64,896]{1,0:T(8,128)(2,1)} %bitcast.10, bf16[2048,896]{1,0:T(8,128)(2,1)} %bitcast.7, ...), custom_call_target="tpu_custom_call" | custom-call | tf_op jit(solution)/shard_map/pallas_call | solution.py:624
  106.7 2.4 %shard_map.95 = (bf16[1,64,896]{2,1,0:T(8,128)(2,1)}, f32[1,64,896]{2,1,0:T(8,128)}, f32[4,112,896]{2,1,0:T(8,128)}) custom-call(bf16[1,64,896]{2,1,0:T(8,128)(2,1)} %bitcast.11, f32[1,64,896]{2,1,0:T(8,128)} %bitcast.8, f32[4,112,896]{2,1,0:T(8,128)} %get-tuple-element.8.refs_2_), custom_call_target="tpu_custom_call" | custom-call | tf_op jit(solution)/shard_map/pallas_call | solution.py:682

commit v4 on v3

--- a/solution.py
+++ b/solution.py
@@ -12,8 +12,9 @@
 MESH = pl.DeviceIdType.MESH
 NX, NY = 4, 4
 SHIFTS = (2, 1, 3)
-SEND_SLOTS = 64
-RECV_SLOTS = 200
+SEND_SLOTS = 40
+Z_FIRST = (0, 2)
+RECV_SLOTS = 88
 SYS_STEPS = tuple((dz, dx) for dx in (2, 1, 3, 0) for dz in (1, 0) if (dz, dx) != (0, 0))
 EDGE_STEPS = tuple((dy, dz) for dy in (2, 1, 3, 0) for dz in (1, 0) if (dy, dz) != (0, 0))
 
@@ -29,24 +30,25 @@
 def kernel(
     chunks,
     experts_hbm,
-    coef,
+    coef_hbm,
     atoms_hbm,
     cot_hbm,
     radial_hbm,
-    src_rows,
-    tgt_rows,
-    src_line,
-    tgt_line,
+    src_rows_hbm,
+    tgt_rows_hbm,
+    src_line_hbm,
+    tgt_line_hbm,
     node_hbm,
     atom_hbm,
     expert_hbm,
     node_out,
     atom_grad,
     expert_grad,
-    atom_total,
-    atom_send,
-    atom_z,
-    atom_d,
+    coef,
+    src_rows,
+    tgt_rows,
+    src_line,
+    tgt_line,
     experts,
     radial,
     at_all,
@@ -67,7 +69,6 @@
     n_atoms = 16 * own_atoms
     n_edges = radial.shape[0]
     n = len(chunks)
-    direct = n - 2
     sys_id = lax.axis_index("sys")
     edge_id = lax.axis_index("edge")
     zh, x = sys_id // NX, sys_id % NX
@@ -98,7 +99,14 @@
         fetch(cot_hbm.at[:, start : start + size], per_chunk[k]["cots"].at[y, zl, c])
         for k, (start, size) in enumerate(chunks)
     ]
+    coef_in = fetch(coef_hbm, coef)
     experts_in = fetch(experts_hbm, experts)
+    index_in = [
+        fetch(src_rows_hbm, src_rows),
+        fetch(tgt_rows_hbm, tgt_rows),
+        fetch(src_line_hbm, src_line),
+        fetch(tgt_line_hbm, tgt_line),
+    ]
     radial_in = fetch(radial_hbm, radial)
 
     barrier = pltpu.get_barrier_semaphore()
@@ -107,23 +115,48 @@
         pl.semaphore_signal(barrier, inc=1, device_id=p, device_id_type=MESH)
     pl.semaphore_wait(barrier, len(peers))
 
-    sent = []
+    sent, groups = [], []
+
+    class Group:
+        def __init__(self, copies, landing):
+            i = len(groups)
+            groups.append(self)
+            for src, dst, peer in copies:
+                j = len(sent)
+                if j >= SEND_SLOTS:
+                    sent[j - SEND_SLOTS].wait_send()
+                cp = pltpu.make_async_remote_copy(
+                    src_ref=src,
+                    dst_ref=dst,
+                    send_sem=send_sem.at[j % SEND_SLOTS],
+                    recv_sem=recv_sem.at[i],
+                    device_id=peer,
+                    device_id_type=MESH,
+                )
+                cp.start()
+                sent.append(cp)
+            self.all = pltpu.make_async_remote_copy(
+                src_ref=landing,
+                dst_ref=landing,
+                send_sem=send_sem.at[0],
+                recv_sem=recv_sem.at[i],
+                device_id=c_peer,
+                device_id_type=MESH,
+            )
+
+        def wait_recv(self):
+            self.all.wait_recv()
 
     def send(src, dst, peer):
-        i = len(sent)
-        if i >= SEND_SLOTS:
-            sent[i - SEND_SLOTS].wait_send()
-        cp = pltpu.make_async_remote_copy(
-            src_ref=src,
-            dst_ref=dst,
-            send_sem=send_sem.at[i % SEND_SLOTS],
-            recv_sem=recv_sem.at[i],
-            device_id=peer,
-            device_id_type=MESH,
-        )
-        cp.start()
-        sent.append(cp)
-        return cp
+        return Group([(src, dst, peer)], dst)
+
+    def send_all(block_of, landing, peers):
+        return [Group([(block_of(*p), landing.at[i], peer) for i, (p, peer) in enumerate(peers)], landing)]
+
+    y_peers = [((d,), y_peer(d)) for d in SHIFTS]
+    x_peers = [((dx,), sys_peer(0, dx)) for dx in SHIFTS]
+    edge_peers = [((dy, dz), edge_peer(dy, dz)) for dy, dz in EDGE_STEPS]
+    sys_peers = [((dz, dx), sys_peer(dz, dx)) for dz, dx in SYS_STEPS]
 
     def share(full, cut):
         lo = full.at[:, :, :, 0:cut]
@@ -132,15 +165,15 @@
         if cut < full.shape[3]:
             m["hi"] = full.at[:, :, :, cut : full.shape[3]]
             block = m["hi"].at[y, zl, c]
-            m["yh"] = [send(block, block, y_peer(d)) for d in SHIFTS]
+            m["yh"] = [Group([(block, block, p) for _, p in y_peers], m["hi"].at[0:3, 0, 0])]
         m["z"] = send(own, own, z_peer)
-        m["y"] += [send(own, own, y_peer(d)) for d in SHIFTS]
+        m["y"].append(Group([(own, own, p) for _, p in y_peers], lo.at[0:3, 0, 0]))
         return m
 
     def share_forward(m):
         m["z"].wait_recv()
         other = m["lo"].at[y, 1 - zl, c]
-        m["y"] += [send(other, other, y_peer(d)) for d in SHIFTS]
+        m["y"].append(Group([(other, other, p) for _, p in y_peers], m["lo"].at[0:3, 0, 0]))
 
     def share_across(m):
         for cp in m["yh"]:
@@ -170,12 +203,11 @@
                     total += coef[to, sys_id * n_exp + e] * experts[e, :, start : start + size].astype(F32)
                 b["epart"][i, z] = total.astype(BF16)
         if k == 0:
-            e_z[0] = [
-                send(b["epart"].at[(SHIFTS + (0,)).index(dx), (zh + dz) % 2], b["ez"].at[i], sys_peer(dz, dx))
-                for i, (dz, dx) in enumerate(SYS_STEPS)
-            ]
+            e_z[0] = send_all(
+                lambda dz, dx: b["epart"].at[(SHIFTS + (0,)).index(dx), (zh + dz) % 2], b["ez"], sys_peers
+            )
         else:
-            e_x[k] = [send(b["epart"].at[i], b["erecv"].at[i], sys_peer(0, dx)) for i, dx in enumerate(SHIFTS)]
+            e_x[k] = send_all(lambda dx: b["epart"].at[SHIFTS.index(dx)], b["erecv"], x_peers)
 
     def expert_x(k):
         b = per_chunk[k]
@@ -193,7 +225,7 @@
             cp.wait_recv()
         own = b["epart"].at[3] if k == 0 else b["esum"]
         total = own[pl.ds(zh, 1)][0].astype(F32)
-        for i in range(len(e_z[k])):
+        for i in range(b["ez"].shape[0]):
             total += b["ez"][i].astype(F32)
         b["merged"][pl.ds(y, 1), pl.ds(zl, 1), pl.ds(c, 1)] = total.astype(BF16)[None, None, None]
         merged_at[k] = share(b["merged"], 48 if k == 0 else rows)
@@ -202,16 +234,18 @@
 
     def merge_forward(k):
         share_forward(merged_at[k])
-        if k > 0:
-            share_forward(cots_at[k])
+        share_forward(cots_at[k])
 
     def merge_core(k):
         share_core(merged_at[k])
-        if k > 0:
-            share_core(cots_at[k])
+
+    def cots_core(k):
+        share_core(cots_at[k])
 
     def merge_wait(k):
         share_wait(merged_at[k])
+
+    def cots_wait(k):
         share_wait(cots_at[k])
 
     def one_hots():
@@ -297,21 +331,17 @@
         if c_recv[k] is None:
             c_recv[k] = []
         for d in tiles:
-            yy = (y + d) % NY
-            at = pl.ds(pl.multiple_of(yy * 256, 256), 256)
+            pair = (y // 2 + d) % 2
+            at = pl.ds(pl.multiple_of(pair * (n_atoms // 2), n_atoms // 2), n_atoms // 2)
             o_s, o_t = ot_src[at, :], ot_tgt[at, :]
             by_src = dot(o_s, edge_vals[:, 0:size]).astype(BF16)
             by_tgt = dot(o_t, edge_vals[:, 0 : 2 * size]).astype(BF16)
-            spot = pl.ds(yy, 1)
-            b["sums"][spot, :, :, :, 0:size] = by_src.reshape(1, 2, 2, own_atoms, size)
-            b["sums"][spot, :, :, :, size : 3 * size] = by_tgt.reshape(1, 2, 2, own_atoms, 2 * size)
-            c_recv[k].append((d, send(b["sums"].at[yy], b["csums"].at[yy], c_peer)))
+            spot = pl.ds(pair * 2, 2)
+            b["sums"][spot, :, :, :, 0:size] = by_src.reshape(2, 2, 2, own_atoms, size)
+            b["sums"][spot, :, :, :, size : 3 * size] = by_tgt.reshape(2, 2, 2, own_atoms, 2 * size)
+            c_recv[k].append((pair, send(b["sums"].at[spot], b["csums"].at[spot], c_peer)))
 
     w_z, w_y, g_z, g_y, n_y, n_z, d_z, d_x = ([None] * n for _ in range(8))
-    a_yz = []
-
-    def to_edge(block_of, landing):
-        return [send(block_of(dy, dz), landing.at[i], edge_peer(dy, dz)) for i, (dy, dz) in enumerate(EDGE_STEPS)]
 
     def atoms_of(dy, dz):
         return (y + dy) % NY, (zl + dz) % 2
@@ -319,18 +349,16 @@
     def reduce_core(k):
         size = chunks[k][1]
         b = per_chunk[k]
-        for d, cp in c_recv[k]:
+        for pair, cp in c_recv[k]:
             cp.wait_recv()
-            spot = pl.ds((y + d) % NY, 1)
+            spot = pl.ds(pair * 2, 2)
             both = b["sums"][spot, :, :, :, 0 : 2 * size].astype(F32) + b["csums"][spot, :, :, :, 0 : 2 * size].astype(F32)
             b["chip"][spot] = both.astype(BF16)
         grad = dot(sel_atoms[...], b["chip"][...].reshape(n_atoms, 2 * size)).astype(BF16)
         b["wpart"][0:2] = grad[:, 0:size].reshape(2, 2, rows, size)
         b["wpart"][2:4] = grad[:, size : 2 * size].reshape(2, 2, rows, size)
-        if k >= direct:
-            w_y[k] = to_edge(lambda dy, dz: b["wpart"].at[atoms_of(dy, dz)], b["wd"])
-            if k < n - 1:
-                g_z[k] = send(b["chip"].at[:, 1 - zl, c], b["gz"], z_peer)
+        if k > 1:
+            w_y[k] = send_all(lambda dy, dz: b["wpart"].at[atoms_of(dy, dz)], b["wd"], edge_peers)
         else:
             w_z[k] = send(b["wpart"].at[:, 1 - zl], b["wz"], z_peer)
 
@@ -340,7 +368,7 @@
         spot = (slice(None), slice(None), pl.ds(c, 1), slice(None), slice(2 * size, 3 * size))
         both = b["sums"][spot].astype(F32) + b["csums"][spot].astype(F32)
         b["nchip"][...] = both.astype(BF16).reshape(NY, 2, own_atoms, size)
-        n_y[k] = [send(b["nchip"].at[(y + d) % NY], b["ny"].at[i], y_peer(d)) for i, d in enumerate(SHIFTS)]
+        n_y[k] = send_all(lambda d: b["nchip"].at[(y + d) % NY], b["ny"], y_peers)
 
     def node_z(k):
         b = per_chunk[k]
@@ -359,63 +387,52 @@
         total = b["nsum"][pl.ds(zl, 1)][0].astype(F32) + b["nz"][...].astype(F32)
         node_out[:, start : start + size] = total.astype(BF16)
 
-    def atom_part(k):
+    def atom_send(k):
+        b = per_chunk[k]
+        if k in Z_FIRST:
+            g_z[k] = send(b["chip"].at[:, 1 - zl, c], b["gz"], z_peer)
+        elif k < 3:
+            g_y[k] = send_all(lambda d: b["chip"].at[(y + d) % NY, :, c], b["gd"], y_peers)
+        else:
+            g_y[k] = send_all(lambda dy, dz: b["chip"].at[(*atoms_of(dy, dz), c)], b["gd"], edge_peers)
+
+    def atom_forward(k):
         size = chunks[k][1]
         b = per_chunk[k]
-        g = b["chip"][:, :, pl.ds(c, 1)].reshape(n_atoms // 2, 2 * size)
-        grad = dot_t(g[:, 0:size], b["merged"][0:2].reshape(width, size))
-        grad += dot_t(g[:, size : 2 * size], b["merged"][2:4].reshape(width, size))
-        grad = grad.reshape(NY, 2, own_atoms, width)
-        if k == 0:
-            atom_total[...] = grad
+        if k in Z_FIRST:
+            g_z[k].wait_recv()
+            own = b["chip"][:, pl.ds(zl, 1), pl.ds(c, 1)].reshape(NY, own_atoms, 2 * size)
+            b["gsum"][...] = (own.astype(F32) + b["gz"][...].astype(F32)).astype(BF16)
+            g_y[k] = send_all(lambda d: b["gsum"].at[(y + d) % NY], b["gd"], y_peers)
         else:
-            atom_total[...] += grad
-        if k == direct - 1:
-            atom_send[...] = atom_total[...].astype(BF16)
-            a_yz.extend(send(atom_send.at[(y + d) % NY], atom_d.at[i], y_peer(d)) for i, d in enumerate(SHIFTS))
-
-    def atom_y():
-        for cp in a_yz:
-            cp.wait_recv()
-        a_yz.clear()
-        total = atom_total[pl.ds(y, 1)][0]
-        for i in range(3):
-            total += atom_d[i].astype(F32)
-        atom_send[pl.ds(y, 1)] = total.astype(BF16)[None]
-        a_yz.append(send(atom_send.at[y, 1 - zl], atom_z, z_peer))
-        atom_total[pl.ds(y, 1)] = total[None]
-
-    def atom_finish():
-        a_yz.pop().wait_recv()
-        atom_grad[...] = atom_total[pl.ds(y, 1), pl.ds(zl, 1)].reshape(own_atoms, width) + atom_z[...].astype(F32)
-
-    def atom_direct(k):
-        b = per_chunk[k]
-        g_y[k] = to_edge(lambda dy, dz: b["chip"].at[(*atoms_of(dy, dz), c)], b["gd"])
-
-    def atom_staged(k):
+            g_y[k][0].wait_recv()
+            total = b["chip"][pl.ds(y, 1), :, pl.ds(c, 1)].reshape(2, own_atoms, 2 * size).astype(F32)
+            for i in range(3):
+                total += b["gd"][i].astype(F32)
+            b["gsum"][...] = total.astype(BF16)
+            g_z[k] = send(b["gsum"].at[1 - zl], b["gz"].at[0], z_peer)
+
+    def atom_finish(k):
         size = chunks[k][1]
         b = per_chunk[k]
-        g_z[k].wait_recv()
-        own = b["chip"][:, pl.ds(zl, 1), pl.ds(c, 1)].reshape(NY, own_atoms, 2 * size)
-        b["gsum"][...] = (own.astype(F32) + b["gz"][...].astype(F32)).astype(BF16)
-        g_y[k] = [send(b["gsum"].at[(y + d) % NY], b["gd"].at[i], y_peer(d)) for i, d in enumerate(SHIFTS)]
-
-    def atom_last(k):
-        size = chunks[k][1]
-        b = per_chunk[k]
-        for cp in g_y[k]:
-            cp.wait_recv()
-        if k == n - 1:
-            total = b["chip"][pl.ds(y, 1), pl.ds(zl, 1), pl.ds(c, 1)][0, 0, 0].astype(F32)
+        if k not in Z_FIRST and k < 3:
+            g_z[k].wait_recv()
+            total = b["gsum"][pl.ds(zl, 1)][0].astype(F32) + b["gz"][0].astype(F32)
         else:
-            total = b["gsum"][pl.ds(y, 1)][0].astype(F32)
-        for i in range(len(g_y[k])):
-            total += b["gd"][i].astype(F32)
+            g_y[k][0].wait_recv()
+            if k in Z_FIRST:
+                total = b["gsum"][pl.ds(y, 1)][0].astype(F32)
+            else:
+                total = b["chip"][pl.ds(y, 1), pl.ds(zl, 1), pl.ds(c, 1)][0, 0, 0].astype(F32)
+            for i in range(b["gd"].shape[0]):
+                total += b["gd"][i].astype(F32)
         g = total.astype(BF16)
         grad = dot_t(g[:, 0:size], b["merged"][0:2].reshape(width, size))
         grad += dot_t(g[:, size : 2 * size], b["merged"][2:4].reshape(width, size))
-        atom_grad[...] += grad
+        if k == 0:
+            atom_grad[...] = grad
+        else:
+            atom_grad[...] += grad
 
     def weight_z(k):
         size = chunks[k][1]
@@ -423,30 +440,30 @@
         w_z[k].wait_recv()
         own = b["wpart"][:, pl.ds(zl, 1)].reshape(NY, rows, size)
         b["wsum"][...] = (own.astype(F32) + b["wz"][...].astype(F32)).astype(BF16)
-        w_y[k] = [send(b["wsum"].at[(y + d) % NY], b["wd"].at[i], y_peer(d)) for i, d in enumerate(SHIFTS)]
+        w_y[k] = send_all(lambda d: b["wsum"].at[(y + d) % NY], b["wd"], y_peers)
 
     def weight_finish(k):
         b = per_chunk[k]
         for cp in w_y[k]:
             cp.wait_recv()
-        if k >= direct:
+        if k > 1:
             total = b["wpart"][pl.ds(y, 1), pl.ds(zl, 1)][0].astype(F32)
         else:
             total = b["wsum"][pl.ds(y, 1)].astype(F32)
-        for i in range(len(w_y[k])):
+        for i in range(b["wd"].shape[0]):
             total += b["wd"][i : i + 1].astype(F32)
         b["dall"][pl.ds(sys_id, 1)] = total.astype(BF16)
         own = b["dall"].at[sys_id]
         if k == n - 1:
-            d_x[k] = [send(own, own, sys_peer(dz, dx)) for dz, dx in SYS_STEPS]
+            d_x[k] = [Group([(own, own, p) for _, p in sys_peers], b["dall"].at[0:7])]
         else:
             d_z[k] = send(own, own, sys_peer(1, 0))
-            d_x[k] = [send(own, own, sys_peer(0, dx)) for dx in SHIFTS]
+            d_x[k] = [Group([(own, own, p) for _, p in x_peers], b["dall"].at[0:3])]
 
     def expert_forward(k):
         d_z[k].wait_recv()
         other = per_chunk[k]["dall"].at[(1 - zh) * NX + x]
-        d_x[k] += [send(other, other, sys_peer(0, dx)) for dx in SHIFTS]
+        d_x[k].append(Group([(other, other, p) for _, p in x_peers], per_chunk[k]["dall"].at[0:3]))
 
     def expert_finish(k):
         start, size = chunks[k]
@@ -467,9 +484,12 @@
     for cp in cot_in:
         cp.wait()
     cots_at[0] = share(per_chunk[0]["cots"], own_atoms // 2)
+    coef_in.wait()
     experts_in.wait()
     for k in range(n):
         expert_part(k)
+    for cp in index_in:
+        cp.wait()
     one_hots()
     share_forward(atoms_at)
     share_forward(cots_at[0])
@@ -485,65 +505,68 @@
     select_atoms()
     share_core(merged_at[0])
     radial_in.wait()
+    merge(1)
+    cots_wait(0)
     merge_wait(0)
 
     work = (
-        (project,),
-        (lambda k: pick(k, 0),),
-        (lambda k: pick(k, 1),),
-        (lambda k: sums(k, SHIFTS[0:1]),),
-        (lambda k: sums(k, SHIFTS[1:2]),),
-        (lambda k: sums(k, SHIFTS[2:3]),),
-        (lambda k: sums(k, (0,)),),
+        project,
+        lambda k: pick(k, 0),
+        lambda k: pick(k, 1),
+        lambda k: sums(k, (1,)),
+        lambda k: sums(k, (0,)),
     )
     beside = {
-        (0, 0): ((merge, 1), (expert_x, 2)),
+        (0, 0): ((expert_x, 2),),
         (0, 1): ((merge_forward, 1),),
-        (0, 2): ((merge, 2),),
-        (0, 4): ((merge_core, 1),),
-        (0, 5): ((merge_forward, 2), (expert_x, 3)),
-        (0, 6): ((merge_wait, 1),),
-        (1, 0): ((reduce_core, 0), (node_core, 0), (atom_part, 0)),
-        (1, 1): ((merge, 3),),
-        (1, 2): ((merge_core, 2),),
-        (1, 4): ((merge_wait, 2),),
-        (1, 5): ((merge_forward, 3), (weight_z, 0)),
-        (2, 0): ((reduce_core, 1), (node_core, 1), (atom_part, 1)),
-        (2, 2): ((merge_core, 3), (weight_finish, 0)),
-        (2, 3): ((node_z, 0),),
-        (2, 4): ((merge_wait, 3),),
-        (2, 5): ((weight_z, 1),),
-        (2, 6): ((expert_forward, 0),),
-        (3, 0): ((reduce_core, 2), (node_core, 2)),
-        (3, 2): ((weight_finish, 1),),
-        (3, 3): ((node_z, 1),),
+        (0, 2): ((expert_x, 3),),
+        (0, 3): ((merge, 2),),
+        (0, 4): (
+            (merge_core, 1),
+            (cots_core, 1),
+            (merge_forward, 2),
+            (merge, 3),
+            (reduce_core, 0),
+            (node_core, 0),
+            (merge_wait, 1),
+        ),
+        (1, 0): ((cots_wait, 1), (atom_send, 0)),
+        (1, 1): ((merge_forward, 3),),
+        (1, 2): ((merge_core, 2), (cots_core, 2)),
+        (1, 3): ((merge_wait, 2), (cots_wait, 2)),
+        (1, 4): ((weight_z, 0),),
+        (2, 0): ((reduce_core, 1), (node_core, 1), (atom_send, 1), (atom_forward, 0)),
+        (2, 2): ((merge_core, 3), (cots_core, 3), (weight_finish, 0)),
+        (2, 3): ((merge_wait, 3), (cots_wait, 3), (node_z, 0), (weight_z, 1)),
+        (3, 0): ((reduce_core, 2), (atom_send, 2), (node_core, 2), (expert_forward, 0)),
+        (3, 2): ((node_z, 1),),
+        (3, 3): ((weight_finish, 1),),
+        (3, 4): ((atom_forward, 1), (atom_finish, 0)),
     }
     for k in range(n):
-        for slot, (f,) in enumerate(work):
+        for slot, f in enumerate(work):
             f(k)
             for g, i in beside.get((k, slot), ()):
                 g(i)
-            if (k, slot) == (3, 4):
-                atom_y()
     reduce_core(3)
+    weight_finish(2)
     node_core(3)
+    atom_send(3)
+    atom_forward(2)
+    expert_finish(0)
     expert_forward(1)
-    weight_finish(2)
-    atom_direct(3)
-    atom_staged(2)
-    expert_finish(0)
+    node_z(2)
     weight_finish(3)
     expert_forward(2)
-    atom_finish()
+    atom_finish(1)
+    node_z(3)
     expert_finish(1)
-    atom_last(3)
-    node_z(2)
-    node_z(3)
-    atom_last(2)
-    outputs.append(fetch(atom_grad, atom_hbm))
     for k in range(n):
         node_finish(k)
     outputs.append(fetch(node_out, node_hbm))
+    atom_finish(2)
+    atom_finish(3)
+    outputs.append(fetch(atom_grad, atom_hbm))
     expert_finish(2)
     expert_finish(3)
 
@@ -554,7 +577,7 @@
     def drain():
         for cp in sent[-SEND_SLOTS:]:
             cp.wait_send()
-        assert len(sent) == recv_sem.shape[0], len(sent)
+        assert len(groups) == recv_sem.shape[0], len(groups)
 
     finish()
     drain()
@@ -607,19 +630,18 @@
             "ny": vmem(3, 2, own, s),
             "nsum": vmem(2, own, s),
             "nz": vmem(own, s),
-            "gz": vmem(NY if k == 2 else 1, own, 2 * s),
-            "gsum": vmem(NY if k == 2 else 1, own, 2 * s),
-            "gd": vmem(7 if k == 3 else 3, own, 2 * s),
+            "gz": vmem(NY if k in Z_FIRST else 1, own, 2 * s),
+            "gsum": vmem(NY if k in Z_FIRST else 2, own, 2 * s),
+            "gd": vmem(*((3,) if k in Z_FIRST else (3, 2) if k < 3 else (7,)), own, 2 * s),
             "wpart": vmem(NY, 2, rows, s),
             "wz": vmem(NY, rows, s),
             "wsum": vmem(NY, rows, s),
-            "wd": vmem(7, rows, s),
+            "wd": vmem(7 if k > 1 else 3, rows, s),
             "dall": vmem(8, rows, s),
         }
         for k, (_, s) in enumerate(chunks)
     ]
     wide = max(s for _, s in chunks)
-    whole = pl.BlockSpec(memory_space=pltpu.VMEM)
     hbm = pl.BlockSpec(memory_space=pl.ANY)
     node, agrad, egrad = pl.pallas_call(
         functools.partial(kernel, chunks),
@@ -628,26 +650,17 @@
             jax.ShapeDtypeStruct((own, width), F32),
             jax.ShapeDtypeStruct((n_exp, rows, width), F32),
         ),
-        in_specs=[
-            hbm,
-            pl.BlockSpec(memory_space=pltpu.SMEM),
-            hbm,
-            hbm,
-            hbm,
-            whole,
-            whole,
-            whole,
-            whole,
-        ],
+        in_specs=[hbm] * 9,
         out_specs=(hbm, hbm, hbm),
         scratch_shapes=[
             vmem(own, width),
             pltpu.VMEM((own, width), F32),
             pltpu.VMEM((n_exp, rows, width), F32),
-            pltpu.VMEM((NY, 2, own, width), F32),
-            vmem(NY, 2, own, width),
-            vmem(own, width),
-            vmem(3, 2, own, width),
+            pltpu.SMEM(coef.shape, F32),
+            pltpu.VMEM((n_edges // 128, 128), jnp.int32),
+            pltpu.VMEM((n_edges // 128, 128), jnp.int32),
+            pltpu.VMEM((1, n_edges), jnp.int32),
+            pltpu.VMEM((1, n_edges), jnp.int32),
             vmem(n_exp, rows, width),
             vmem(n_edges, width),
             vmem(NY, 2, 2, own, width),
@@ -659,7 +672,7 @@
             vmem(2, n_atoms, wide),
             vmem(n_edges, 2 * wide),
             per_chunk,
-            pltpu.SemaphoreType.DMA((5 + 2 * len(chunks),)),
+            pltpu.SemaphoreType.DMA((10 + 2 * len(chunks),)),
             pltpu.SemaphoreType.DMA((SEND_SLOTS,)),
             pltpu.SemaphoreType.DMA((RECV_SLOTS,)),
         ],

time: 110 us -> 104 us (0.945)
  Pallas kernels: 108 us -> 103 us
    pallas_call x1, Pallas kernels: 106 us -> 100 us  [layer(): pl.pallas_call(functools.partial(kernel, chunks), out_shape=(jax.ShapeDty...]
where the time goes in v4:
time: 104 us
  Pallas kernels  103 us (99%)
    pallas_call x1, Pallas kernels, layer(): pl.pallas_call(functools.partial(kernel, chunks), out_shape=(jax.ShapeDty...  100 us
    pallas_call x1, Pallas kernels, layer(): pl.pallas_call(write_out, out_shape=tuple((jax.ShapeDtypeStruct(r.shape,...  2.42 us

profile of v4, /device:TPU:1, one launch (start us, length us, event | category | flops | bytes accessed | tf_op | source)
XLA Modules:
  0.0 103.7 jit_solution(16791716804644664901)
XLA Ops:
  0.6 100.5 %shard_map.94 = (bf16[64,896]{1,0:T(8,128)(2,1)}, f32[64,896]{1,0:T(8,128)}, f32[4,112,896]{2,1,0:T(8,128)}) custom-call(bf16[4,112,896]{2,1,0:T(8,128)(2,1)} %experts_hbm.1, f32[8,32]{1,0:T(8,128)} %coef_hbm.1, bf16[64,896]{1,0:T(8,128)(2,1)} %bitcast.9, bf16[64,896]{1,0:T(8,128)(2,1)} %bitcast.10, bf16[2048,896]{1,0:T(8,128)(2,1)} %bitcast.7, ...), custom_call_target="tpu_custom_call" | custom-call | tf_op jit(solution)/shard_map/pallas_call | solution.py:646
  101.1 2.4 %shard_map.95 = (bf16[1,64,896]{2,1,0:T(8,128)(2,1)}, f32[1,64,896]{2,1,0:T(8,128)}, f32[4,112,896]{2,1,0:T(8,128)}) custom-call(bf16[1,64,896]{2,1,0:T(8,128)(2,1)} %bitcast.11, f32[1,64,896]{2,1,0:T(8,128)} %bitcast.8, f32[4,112,896]{2,1,0:T(8,128)} %get-tuple-element.8.refs_2_), custom_call_target="tpu_custom_call" | custom-call | tf_op jit(solution)/shard_map/pallas_call | solution.py:695

commit v5 on v4

--- a/solution.py
+++ b/solution.py
@@ -13,8 +13,7 @@
 NX, NY = 4, 4
 SHIFTS = (2, 1, 3)
 SEND_SLOTS = 40
-Z_FIRST = (0, 2)
-RECV_SLOTS = 88
+RECV_SLOTS = 89
 SYS_STEPS = tuple((dz, dx) for dx in (2, 1, 3, 0) for dz in (1, 0) if (dz, dx) != (0, 0))
 EDGE_STEPS = tuple((dy, dz) for dy in (2, 1, 3, 0) for dz in (1, 0) if (dy, dz) != (0, 0))
 
@@ -59,6 +58,7 @@
     sel_atoms,
     proj,
     edge_vals,
+    edge_cots,
     per_chunk,
     local_sem,
     send_sem,
@@ -228,13 +228,16 @@
         for i in range(b["ez"].shape[0]):
             total += b["ez"][i].astype(F32)
         b["merged"][pl.ds(y, 1), pl.ds(zl, 1), pl.ds(c, 1)] = total.astype(BF16)[None, None, None]
-        merged_at[k] = share(b["merged"], 48 if k == 0 else rows)
-        if k > 0:
+        merged_at[k] = share(b["merged"], rows * 3 // 7 if k == 0 else rows)
+        if k > 1:
             cots_at[k] = share(b["cots"], own_atoms)
 
     def merge_forward(k):
+        if k == 1:
+            share_forward(cots_at[k])
         share_forward(merged_at[k])
-        share_forward(cots_at[k])
+        if k > 1:
+            share_forward(cots_at[k])
 
     def merge_core(k):
         share_core(merged_at[k])
@@ -299,6 +302,17 @@
 
         lax.fori_loop(0, NY, body, 0)
 
+    def pick_first():
+        size = chunks[0][1]
+        b = per_chunk[0]
+
+        def body(t, _):
+            at = pl.ds(pl.multiple_of(t * 512, 512), 512)
+            edge_cots[at, :] = dot(oh_tgt[at, :], b["cots"][...].reshape(n_atoms, size)).astype(BF16)
+            return 0
+
+        lax.fori_loop(0, n_edges // 512, body, 0)
+
     def pick(k, half):
         start, size = chunks[k]
         b = per_chunk[k]
@@ -314,7 +328,10 @@
                 pre = dot(o_s, proj[0, :, 0:size]) + by_tgt[:, 0:size]
             else:
                 pre = dot(o_s, proj[0, :, 0:size]) + dot(o_t, proj[1, :, 0:size])
-                edge_cot = dot(o_t, b["cots"][...].reshape(n_atoms, size))
+                if k == 0:
+                    edge_cot = edge_cots[at, :].astype(F32)
+                else:
+                    edge_cot = dot(o_t, b["cots"][...].reshape(n_atoms, size))
             r = radial[at, start : start + size].astype(F32)
             g = 1.0 / (1.0 + jnp.exp(-pre))
             edge_vals[at, 0:size] = (edge_cot * r * (g * (1.0 + pre * (1.0 - g)))).astype(BF16)
@@ -343,6 +360,8 @@
 
     w_z, w_y, g_z, g_y, n_y, n_z, d_z, d_x = ([None] * n for _ in range(8))
 
+    h_y = []
+
     def atoms_of(dy, dz):
         return (y + dy) % NY, (zl + dz) % 2
 
@@ -357,7 +376,7 @@
         grad = dot(sel_atoms[...], b["chip"][...].reshape(n_atoms, 2 * size)).astype(BF16)
         b["wpart"][0:2] = grad[:, 0:size].reshape(2, 2, rows, size)
         b["wpart"][2:4] = grad[:, size : 2 * size].reshape(2, 2, rows, size)
-        if k > 1:
+        if k > 0:
             w_y[k] = send_all(lambda dy, dz: b["wpart"].at[atoms_of(dy, dz)], b["wd"], edge_peers)
         else:
             w_z[k] = send(b["wpart"].at[:, 1 - zl], b["wz"], z_peer)
@@ -387,45 +406,51 @@
         total = b["nsum"][pl.ds(zl, 1)][0].astype(F32) + b["nz"][...].astype(F32)
         node_out[:, start : start + size] = total.astype(BF16)
 
+    def zy_part(k):
+        return chunks[k][1] * (1 if k == 2 else 2)
+
     def atom_send(k):
         b = per_chunk[k]
-        if k in Z_FIRST:
-            g_z[k] = send(b["chip"].at[:, 1 - zl, c], b["gz"], z_peer)
-        elif k < 3:
-            g_y[k] = send_all(lambda d: b["chip"].at[(y + d) % NY, :, c], b["gd"], y_peers)
-        else:
+        part = zy_part(k)
+        if k == 3:
             g_y[k] = send_all(lambda dy, dz: b["chip"].at[(*atoms_of(dy, dz), c)], b["gd"], edge_peers)
+            return
+        g_z[k] = send(b["chip"].at[:, 1 - zl, c, :, 0:part], b["gz"], z_peer)
+        if k == 2:
+            h_y.extend(send_all(lambda d: b["chip"].at[(y + d) % NY, :, c, :, part : 2 * part], b["hd"], y_peers))
 
     def atom_forward(k):
-        size = chunks[k][1]
-        b = per_chunk[k]
-        if k in Z_FIRST:
-            g_z[k].wait_recv()
-            own = b["chip"][:, pl.ds(zl, 1), pl.ds(c, 1)].reshape(NY, own_atoms, 2 * size)
-            b["gsum"][...] = (own.astype(F32) + b["gz"][...].astype(F32)).astype(BF16)
-            g_y[k] = send_all(lambda d: b["gsum"].at[(y + d) % NY], b["gd"], y_peers)
-        else:
-            g_y[k][0].wait_recv()
-            total = b["chip"][pl.ds(y, 1), :, pl.ds(c, 1)].reshape(2, own_atoms, 2 * size).astype(F32)
-            for i in range(3):
-                total += b["gd"][i].astype(F32)
-            b["gsum"][...] = total.astype(BF16)
-            g_z[k] = send(b["gsum"].at[1 - zl], b["gz"].at[0], z_peer)
+        part = zy_part(k)
+        b = per_chunk[k]
+        g_z[k].wait_recv()
+        own = b["chip"][:, pl.ds(zl, 1), pl.ds(c, 1), :, 0:part].reshape(NY, own_atoms, part)
+        b["gsum"][...] = (own.astype(F32) + b["gz"][...].astype(F32)).astype(BF16)
+        g_y[k] = send_all(lambda d: b["gsum"].at[(y + d) % NY], b["gd"], y_peers)
+
+    def atom_across(k):
+        part = zy_part(k)
+        b = per_chunk[k]
+        h_y[0].wait_recv()
+        total = b["chip"][pl.ds(y, 1), :, pl.ds(c, 1), :, part : 2 * part].reshape(2, own_atoms, part).astype(F32)
+        for i in range(3):
+            total += b["hd"][i].astype(F32)
+        b["hsum"][...] = total.astype(BF16)
+        h_y.append(send(b["hsum"].at[1 - zl], b["hz"], z_peer))
 
     def atom_finish(k):
         size = chunks[k][1]
         b = per_chunk[k]
-        if k not in Z_FIRST and k < 3:
-            g_z[k].wait_recv()
-            total = b["gsum"][pl.ds(zl, 1)][0].astype(F32) + b["gz"][0].astype(F32)
+        g_y[k][0].wait_recv()
+        if k < 3:
+            total = b["gsum"][pl.ds(y, 1)][0].astype(F32)
         else:
-            g_y[k][0].wait_recv()
-            if k in Z_FIRST:
-                total = b["gsum"][pl.ds(y, 1)][0].astype(F32)
-            else:
-                total = b["chip"][pl.ds(y, 1), pl.ds(zl, 1), pl.ds(c, 1)][0, 0, 0].astype(F32)
-            for i in range(b["gd"].shape[0]):
-                total += b["gd"][i].astype(F32)
+            total = b["chip"][pl.ds(y, 1), pl.ds(zl, 1), pl.ds(c, 1)][0, 0, 0].astype(F32)
+        for i in range(b["gd"].shape[0]):
+            total += b["gd"][i].astype(F32)
+        if k == 2:
+            h_y[1].wait_recv()
+            rest = b["hsum"][pl.ds(zl, 1)][0].astype(F32) + b["hz"][...].astype(F32)
+            total = jnp.concatenate([total, rest], axis=1)
         g = total.astype(BF16)
         grad = dot_t(g[:, 0:size], b["merged"][0:2].reshape(width, size))
         grad += dot_t(g[:, size : 2 * size], b["merged"][2:4].reshape(width, size))
@@ -446,7 +471,7 @@
         b = per_chunk[k]
         for cp in w_y[k]:
             cp.wait_recv()
-        if k > 1:
+        if k > 0:
             total = b["wpart"][pl.ds(y, 1), pl.ds(zl, 1)][0].astype(F32)
         else:
             total = b["wsum"][pl.ds(y, 1)].astype(F32)
@@ -503,10 +528,12 @@
     share_core(cots_at[0])
     share_wait(atoms_at)
     select_atoms()
+    cots_at[1] = share(per_chunk[1]["cots"], own_atoms)
+    cots_wait(0)
+    pick_first()
     share_core(merged_at[0])
     radial_in.wait()
     merge(1)
-    cots_wait(0)
     merge_wait(0)
 
     work = (
@@ -517,31 +544,21 @@
         lambda k: sums(k, (0,)),
     )
     beside = {
-        (0, 0): ((expert_x, 2),),
-        (0, 1): ((merge_forward, 1),),
+        (0, 0): ((merge_forward, 1), (expert_x, 2)),
         (0, 2): ((expert_x, 3),),
-        (0, 3): ((merge, 2),),
-        (0, 4): (
-            (merge_core, 1),
-            (cots_core, 1),
-            (merge_forward, 2),
-            (merge, 3),
-            (reduce_core, 0),
-            (node_core, 0),
-            (merge_wait, 1),
-        ),
-        (1, 0): ((cots_wait, 1), (atom_send, 0)),
+        (0, 3): ((merge, 2), (merge_core, 1)),
+        (0, 4): ((cots_core, 1), (merge_wait, 1)),
+        (1, 0): ((merge_forward, 2), (merge, 3), (reduce_core, 0), (node_core, 0), (atom_send, 0), (cots_wait, 1)),
         (1, 1): ((merge_forward, 3),),
-        (1, 2): ((merge_core, 2), (cots_core, 2)),
-        (1, 3): ((merge_wait, 2), (cots_wait, 2)),
+        (1, 2): ((merge_core, 2),),
+        (1, 3): ((merge_wait, 2), (cots_core, 2)),
         (1, 4): ((weight_z, 0),),
-        (2, 0): ((reduce_core, 1), (node_core, 1), (atom_send, 1), (atom_forward, 0)),
+        (2, 0): ((cots_wait, 2), (reduce_core, 1), (node_core, 1), (atom_send, 1)),
+        (2, 1): ((atom_forward, 0),),
         (2, 2): ((merge_core, 3), (cots_core, 3), (weight_finish, 0)),
-        (2, 3): ((merge_wait, 3), (cots_wait, 3), (node_z, 0), (weight_z, 1)),
-        (3, 0): ((reduce_core, 2), (atom_send, 2), (node_core, 2), (expert_forward, 0)),
-        (3, 2): ((node_z, 1),),
-        (3, 3): ((weight_finish, 1),),
-        (3, 4): ((atom_forward, 1), (atom_finish, 0)),
+        (2, 3): ((merge_wait, 3), (cots_wait, 3), (node_z, 0)),
+        (3, 0): ((weight_finish, 1), (reduce_core, 2), (atom_send, 2)),
+        (3, 3): ((expert_forward, 0), (node_z, 1)),
     }
     for k in range(n):
         for slot, f in enumerate(work):
@@ -549,22 +566,26 @@
             for g, i in beside.get((k, slot), ()):
                 g(i)
     reduce_core(3)
+    atom_forward(1)
+    expert_forward(1)
     weight_finish(2)
+    node_core(2)
     node_core(3)
     atom_send(3)
+    atom_across(2)
+    atom_finish(0)
+    expert_finish(0)
     atom_forward(2)
-    expert_finish(0)
-    expert_forward(1)
-    node_z(2)
     weight_finish(3)
     expert_forward(2)
     atom_finish(1)
+    node_z(2)
+    expert_finish(1)
     node_z(3)
-    expert_finish(1)
+    atom_finish(2)
     for k in range(n):
         node_finish(k)
     outputs.append(fetch(node_out, node_hbm))
-    atom_finish(2)
     atom_finish(3)
     outputs.append(fetch(atom_grad, atom_hbm))
     expert_finish(2)
@@ -630,13 +651,16 @@
             "ny": vmem(3, 2, own, s),
             "nsum": vmem(2, own, s),
             "nz": vmem(own, s),
-            "gz": vmem(NY if k in Z_FIRST else 1, own, 2 * s),
-            "gsum": vmem(NY if k in Z_FIRST else 2, own, 2 * s),
-            "gd": vmem(*((3,) if k in Z_FIRST else (3, 2) if k < 3 else (7,)), own, 2 * s),
+            "gz": vmem(NY, own, s if k == 2 else 2 * s),
+            "gsum": vmem(NY, own, s if k == 2 else 2 * s),
+            "gd": vmem(3 if k < 3 else 7, own, s if k == 2 else 2 * s),
+            "hd": vmem(3, 2, own, s),
+            "hsum": vmem(2, own, s),
+            "hz": vmem(own, s),
             "wpart": vmem(NY, 2, rows, s),
             "wz": vmem(NY, rows, s),
             "wsum": vmem(NY, rows, s),
-            "wd": vmem(7 if k > 1 else 3, rows, s),
+            "wd": vmem(7 if k > 0 else 3, rows, s),
             "dall": vmem(8, rows, s),
         }
         for k, (_, s) in enumerate(chunks)
@@ -671,6 +695,7 @@
             vmem(4 * rows, n_atoms),
             vmem(2, n_atoms, wide),
             vmem(n_edges, 2 * wide),
+            vmem(n_edges, chunks[0][1]),
             per_chunk,
             pltpu.SemaphoreType.DMA((10 + 2 * len(chunks),)),
             pltpu.SemaphoreType.DMA((SEND_SLOTS,)),

time: 104 us -> 100 us (0.962)
  Pallas kernels: 103 us -> 99.5 us
    pallas_call x1, Pallas kernels: 100 us -> 97.1 us  [layer(): pl.pallas_call(functools.partial(kernel, chunks), out_shape=(jax.ShapeDty...]
where the time goes in v5:
time: 100 us
  Pallas kernels  99.5 us (100%)
    pallas_call x1, Pallas kernels, layer(): pl.pallas_call(functools.partial(kernel, chunks), out_shape=(jax.ShapeDty...  97.1 us
    pallas_call x1, Pallas kernels, layer(): pl.pallas_call(write_out, out_shape=tuple((jax.ShapeDtypeStruct(r.shape,...  2.42 us

profile of v5, /device:TPU:1, one launch (start us, length us, event | category | flops | bytes accessed | tf_op | source)
XLA Modules:
  0.0 100.3 jit_solution(6982927117794151333)
XLA Ops:
  0.6 97.1 %shard_map.94 = (bf16[64,896]{1,0:T(8,128)(2,1)}, f32[64,896]{1,0:T(8,128)}, f32[4,112,896]{2,1,0:T(8,128)}) custom-call(bf16[4,112,896]{2,1,0:T(8,128)(2,1)} %experts_hbm.1, f32[8,32]{1,0:T(8,128)} %coef_hbm.1, bf16[64,896]{1,0:T(8,128)(2,1)} %bitcast.9, bf16[64,896]{1,0:T(8,128)(2,1)} %bitcast.10, bf16[2048,896]{1,0:T(8,128)(2,1)} %bitcast.7, ...), custom_call_target="tpu_custom_call" | custom-call | tf_op jit(solution)/shard_map/pallas_call | solution.py:670
  97.7 2.4 %shard_map.95 = (bf16[1,64,896]{2,1,0:T(8,128)(2,1)}, f32[1,64,896]{2,1,0:T(8,128)}, f32[4,112,896]{2,1,0:T(8,128)}) custom-call(bf16[1,64,896]{2,1,0:T(8,128)(2,1)} %bitcast.11, f32[1,64,896]{2,1,0:T(8,128)} %bitcast.8, f32[4,112,896]{2,1,0:T(8,128)} %get-tuple-element.8.refs_2_), custom_call_target="tpu_custom_call" | custom-call | tf_op jit(solution)/shard_map/pallas_call | solution.py:720

commit v6 on v5

--- a/solution.py
+++ b/solution.py
@@ -13,7 +13,7 @@
 NX, NY = 4, 4
 SHIFTS = (2, 1, 3)
 SEND_SLOTS = 40
-RECV_SLOTS = 89
+RECV_SLOTS = 91
 SYS_STEPS = tuple((dz, dx) for dx in (2, 1, 3, 0) for dz in (1, 0) if (dz, dx) != (0, 0))
 EDGE_STEPS = tuple((dy, dz) for dy in (2, 1, 3, 0) for dz in (1, 0) if (dy, dz) != (0, 0))
 
@@ -56,9 +56,7 @@
     ot_src,
     ot_tgt,
     sel_atoms,
-    proj,
     edge_vals,
-    edge_cots,
     per_chunk,
     local_sem,
     send_sem,
@@ -86,6 +84,7 @@
     z_peer = edge_peer(0, 1)
     c_peer = (sys_id, y * 4 + zl * 2 + (1 - c))
 
+    edge_cots = per_chunk[n - 2]["proj"]
     inputs = []
 
     def fetch(src, dst):
@@ -281,26 +280,41 @@
         pick = jnp.where(j == i + (i // rows + c) * rows, 1.0, 0.0).astype(BF16)
         sel_atoms[...] = dot_t(pick, at_all[...].reshape(n_atoms, width)).astype(BF16)
 
+    p_c = [None] * n
+
+    def projected(k):
+        return per_chunk[k if k >= 2 else n - 1]["proj"]
+
     def project(k):
         size = chunks[k][1]
         b = per_chunk[k]
-        narrow = 2 * size <= proj.shape[2]
-
-        def body(t, _):
+        out = projected(k)
+        narrow = 2 * size <= out.shape[2]
+        first, count = (2 * c, 2) if k >= 2 else (0, NY)
+
+        def body(i, _):
+            t = first + i
             at = pl.ds(pl.multiple_of(t * 256, 256), 256)
             a = at_all[pl.ds(t, 1)].reshape(256, width)
             w = [b["merged"][2 * h : 2 * h + 2].reshape(width, size) for h in range(2)]
             if narrow:
                 both = dot(a, jnp.concatenate(w, axis=1)).astype(BF16)
-                proj[0, at, 0:size] = both[:, 0:size]
-                proj[1, at, 0:size] = both[:, size : 2 * size]
-                proj[1, at, size : 2 * size] = b["cots"][pl.ds(t, 1)].reshape(256, size)
+                out[0, at, 0:size] = both[:, 0:size]
+                out[1, at, 0:size] = both[:, size : 2 * size]
             else:
                 for h in range(2):
-                    proj[h, at, 0:size] = dot(a, w[h]).astype(BF16)
+                    out[h, at, 0:size] = dot(a, w[h]).astype(BF16)
             return 0
 
-        lax.fori_loop(0, NY, body, 0)
+        lax.fori_loop(0, count, body, 0)
+        if k >= 2:
+            own = out.at[:, pl.ds(pl.multiple_of(c * (n_atoms // 2), 512), n_atoms // 2), 0:size]
+            p_c[k] = send(own, own, c_peer)
+        if narrow:
+            out[1, :, size : 2 * size] = b["cots"][...].reshape(n_atoms, size)
+
+    def project_wait(k):
+        p_c[k].wait_recv()
 
     def pick_first():
         size = chunks[0][1]
@@ -308,7 +322,9 @@
 
         def body(t, _):
             at = pl.ds(pl.multiple_of(t * 512, 512), 512)
-            edge_cots[at, :] = dot(oh_tgt[at, :], b["cots"][...].reshape(n_atoms, size)).astype(BF16)
+            edge_cots[t // 2, pl.ds(pl.multiple_of((t % 2) * 512, 512), 512), :] = dot(
+                oh_tgt[at, :], b["cots"][...].reshape(n_atoms, size)
+            ).astype(BF16)
             return 0
 
         lax.fori_loop(0, n_edges // 512, body, 0)
@@ -316,20 +332,21 @@
     def pick(k, half):
         start, size = chunks[k]
         b = per_chunk[k]
-        narrow = 2 * size <= proj.shape[2]
+        pr = projected(k)
+        narrow = 2 * size <= pr.shape[2]
         count = n_edges // 1024
 
         def body(t, _):
             at = pl.ds(pl.multiple_of(t * 512, 512), 512)
             o_s, o_t = oh_src[at, :], oh_tgt[at, :]
             if narrow:
-                by_tgt = dot(o_t, proj[1, :, 0 : 2 * size])
+                by_tgt = dot(o_t, pr[1, :, 0 : 2 * size])
                 edge_cot = by_tgt[:, size : 2 * size]
-                pre = dot(o_s, proj[0, :, 0:size]) + by_tgt[:, 0:size]
+                pre = dot(o_s, pr[0, :, 0:size]) + by_tgt[:, 0:size]
             else:
-                pre = dot(o_s, proj[0, :, 0:size]) + dot(o_t, proj[1, :, 0:size])
+                pre = dot(o_s, pr[0, :, 0:size]) + dot(o_t, pr[1, :, 0:size])
                 if k == 0:
-                    edge_cot = edge_cots[at, :].astype(F32)
+                    edge_cot = edge_cots[t // 2, pl.ds(pl.multiple_of((t % 2) * 512, 512), 512), :].astype(F32)
                 else:
                     edge_cot = dot(o_t, b["cots"][...].reshape(n_atoms, size))
             r = radial[at, start : start + size].astype(F32)
@@ -537,7 +554,7 @@
     merge_wait(0)
 
     work = (
-        project,
+        lambda k: project_wait(k) if k >= 2 else project(k),
         lambda k: pick(k, 0),
         lambda k: pick(k, 1),
         lambda k: sums(k, (1,)),
@@ -551,14 +568,15 @@
         (1, 0): ((merge_forward, 2), (merge, 3), (reduce_core, 0), (node_core, 0), (atom_send, 0), (cots_wait, 1)),
         (1, 1): ((merge_forward, 3),),
         (1, 2): ((merge_core, 2),),
-        (1, 3): ((merge_wait, 2), (cots_core, 2)),
+        (1, 3): ((merge_wait, 2), (project, 2), (cots_core, 2)),
         (1, 4): ((weight_z, 0),),
-        (2, 0): ((cots_wait, 2), (reduce_core, 1), (node_core, 1), (atom_send, 1)),
-        (2, 1): ((atom_forward, 0),),
+        (2, 0): ((cots_wait, 2),),
+        (2, 1): ((reduce_core, 1), (node_core, 1), (atom_send, 1), (atom_forward, 0)),
         (2, 2): ((merge_core, 3), (cots_core, 3), (weight_finish, 0)),
-        (2, 3): ((merge_wait, 3), (cots_wait, 3), (node_z, 0)),
-        (3, 0): ((weight_finish, 1), (reduce_core, 2), (atom_send, 2)),
-        (3, 3): ((expert_forward, 0), (node_z, 1)),
+        (2, 3): ((merge_wait, 3), (cots_wait, 3), (project, 3), (node_z, 0)),
+        (3, 1): ((reduce_core, 2), (atom_send, 2)),
+        (3, 2): ((weight_finish, 1),),
+        (3, 3): ((node_z, 1),),
     }
     for k in range(n):
         for slot, f in enumerate(work):
@@ -567,11 +585,12 @@
                 g(i)
     reduce_core(3)
     atom_forward(1)
-    expert_forward(1)
-    weight_finish(2)
     node_core(2)
     node_core(3)
+    expert_forward(0)
+    weight_finish(2)
     atom_send(3)
+    expert_forward(1)
     atom_across(2)
     atom_finish(0)
     expert_finish(0)
@@ -636,11 +655,14 @@
     def vmem(*shape):
         return pltpu.VMEM(shape, BF16)
 
+    def vmem_if(used, *shape):
+        return vmem(*shape) if used else vmem(16, 128)
+
     per_chunk = [
         {
             "epart": vmem(4, 2, rows, s),
-            "erecv": vmem(3, 2, rows, s),
-            "esum": vmem(2, rows, s),
+            "erecv": vmem_if(k > 0, 3, 2, rows, s),
+            "esum": vmem_if(k > 0, 2, rows, s),
             "ez": vmem(7 if k == 0 else 1, rows, s),
             "cots": vmem(NY, 2, 2, own, s),
             "merged": vmem(NY, 2, 2, rows, s),
@@ -651,17 +673,18 @@
             "ny": vmem(3, 2, own, s),
             "nsum": vmem(2, own, s),
             "nz": vmem(own, s),
-            "gz": vmem(NY, own, s if k == 2 else 2 * s),
-            "gsum": vmem(NY, own, s if k == 2 else 2 * s),
+            "gz": vmem_if(k < 3, NY, own, s if k == 2 else 2 * s),
+            "gsum": vmem_if(k < 3, NY, own, s if k == 2 else 2 * s),
             "gd": vmem(3 if k < 3 else 7, own, s if k == 2 else 2 * s),
-            "hd": vmem(3, 2, own, s),
-            "hsum": vmem(2, own, s),
-            "hz": vmem(own, s),
+            "hd": vmem_if(k == 2, 3, 2, own, s),
+            "hsum": vmem_if(k == 2, 2, own, s),
+            "hz": vmem_if(k == 2, own, s),
             "wpart": vmem(NY, 2, rows, s),
-            "wz": vmem(NY, rows, s),
-            "wsum": vmem(NY, rows, s),
+            "wz": vmem_if(k == 0, NY, rows, s),
+            "wsum": vmem_if(k == 0, NY, rows, s),
             "wd": vmem(7 if k > 0 else 3, rows, s),
             "dall": vmem(8, rows, s),
+            "proj": vmem_if(k >= 2, 2, n_atoms, 256),
         }
         for k, (_, s) in enumerate(chunks)
     ]
@@ -693,9 +716,7 @@
             vmem(n_atoms, n_edges),
             vmem(n_atoms, n_edges),
             vmem(4 * rows, n_atoms),
-            vmem(2, n_atoms, wide),
             vmem(n_edges, 2 * wide),
-            vmem(n_edges, chunks[0][1]),
             per_chunk,
             pltpu.SemaphoreType.DMA((10 + 2 * len(chunks),)),
             pltpu.SemaphoreType.DMA((SEND_SLOTS,)),

time: 100 us -> 98.1 us (0.981)
  Pallas kernels: 99.5 us -> 97.1 us
    pallas_call x1, Pallas kernels: 97.1 us -> 94.7 us  [layer(): pl.pallas_call(functools.partial(kernel, chunks), out_shape=(jax.ShapeDty...]
where the time goes in v6:
time: 98.1 us; the launch traced here: 97.9 us
  Pallas kernels  97.1 us (99%)
    pallas_call x1, Pallas kernels, layer(): pl.pallas_call(functools.partial(kernel, chunks), out_shape=(jax.ShapeDty...  94.7 us
    pallas_call x1, Pallas kernels, layer(): pl.pallas_call(write_out, out_shape=tuple((jax.ShapeDtypeStruct(r.shape,...  2.42 us

profile of v6, /device:TPU:1, one launch (start us, length us, event | category | flops | bytes accessed | tf_op | source)
XLA Modules:
  0.0 97.9 jit_solution(5169934366109188019)
XLA Ops:
  0.6 94.7 %shard_map.94 = (bf16[64,896]{1,0:T(8,128)(2,1)}, f32[64,896]{1,0:T(8,128)}, f32[4,112,896]{2,1,0:T(8,128)}) custom-call(bf16[4,112,896]{2,1,0:T(8,128)(2,1)} %experts_hbm.1, f32[8,32]{1,0:T(8,128)} %coef_hbm.1, bf16[64,896]{1,0:T(8,128)(2,1)} %bitcast.9, bf16[64,896]{1,0:T(8,128)(2,1)} %bitcast.10, bf16[2048,896]{1,0:T(8,128)(2,1)} %bitcast.7, ...), custom_call_target="tpu_custom_call" | custom-call | tf_op jit(solution)/shard_map/pallas_call | solution.py:693
  95.3 2.4 %shard_map.95 = (bf16[1,64,896]{2,1,0:T(8,128)(2,1)}, f32[1,64,896]{2,1,0:T(8,128)}, f32[4,112,896]{2,1,0:T(8,128)}) custom-call(bf16[1,64,896]{2,1,0:T(8,128)(2,1)} %bitcast.11, f32[1,64,896]{2,1,0:T(8,128)} %bitcast.8, f32[4,112,896]{2,1,0:T(8,128)} %get-tuple-element.8.refs_2_), custom_call_target="tpu_custom_call" | custom-call | tf_op jit(solution)/shard_map/pallas_call | solution.py:741
